TPU v7x, 512 devices: a whole 4x4x16 slice. The times are simulated.
512 devices in a mesh: vox: 16 (over x_hi, y, core), filt: 32 (over x_lo, z).
Axes of the slice: x: 4 (x_hi: 2, x_lo: 2; x = x_hi * 2 + x_lo), y: 4, z: 16, core: 2. Of those that a mesh axis runs over, the one named last changes fastest.
Arguments:
- volume: bfloat16 [1024, 64, 128], P('filt', 'vox'), may hold values from -6 to 6
- kernel: bfloat16 [27, 1024, 1024], P(None, 'filt', 'vox'), may hold values from -0.0390625 to 0.0390625
- bias: float32 [1024], P('filt'), may hold values from -3 to 3
Outputs:
- features: bfloat16 [1024, 64, 128], P('filt', 'vox')
All inputs are finite; a program needn't handle non-finite values.
Results may differ from a plain program's by a relative error of at most 0.001.
Values may be sent and summed in bfloat16 or wider, within the bound.
No kernel may reach another device: no remote copies, remote signals or barrier semaphores. Data moves between devices by JAX's collectives and lax.ppermute only.
A program may use at most 64 MiB of HBM per device.

v0:
```python
import jax
import jax.numpy as jnp
from jax import lax
from jax.sharding import PartitionSpec as P

H = 4
W = 32


def padded(block, sides, width):
    for axis, dim in sides:
        count = lax.axis_size(axis)
        forward = [(i, i + 1) for i in range(count - 1)]
        backward = [(target, source) for source, target in forward]
        low = lax.ppermute(
            lax.slice_in_dim(block, block.shape[dim] - width, None, axis=dim), axis, forward
        )
        high = lax.ppermute(lax.slice_in_dim(block, 0, width, axis=dim), axis, backward)
        block = jnp.concatenate([low, block, high], axis=dim)
    return block


def convolve(planes, weights):
    channels = planes.shape[0]
    stack = planes.shape[1]
    filters = weights.shape[3]
    shaped = planes.reshape(1, channels, stack, H, W)
    summed = lax.conv_general_dilated(
        shaped,
        weights,
        (1, 1, 1),
        [(0, 0), (1, 1), (1, 1)],
        dimension_numbers=("NCDHW", "DHWOI", "NCDHW"),
        preferred_element_type=jnp.float32,
    )
    return summed[0].reshape(filters, stack - 2, H * W)


def shards(volume, kernel, bias):
    gathered = lax.all_gather(kernel, "vox", axis=2, tiled=True)
    filters = gathered.shape[1]
    kernel_taps = gathered.reshape(3, 3, 3, filters, gathered.shape[2])
    rimmed = padded(volume, (("vox", 1),), 1)
    whole_rimmed = lax.all_gather(rimmed, "filt", axis=0, tiled=True)
    summed = convolve(whole_rimmed, kernel_taps)
    return (summed + bias[:, None, None]).astype(jnp.bfloat16)


def solution(mesh):
    in_specs = (P("filt", "vox", None), P(None, "filt", "vox"), P("filt"))
    out_specs = P("filt", "vox", None)
    return jax.shard_map(shards, mesh=mesh, in_specs=in_specs, out_specs=out_specs, check_vma=False)
```

profile of v0, /device:TPU:1, one launch (start us, length us, event | category | flops | bytes accessed | tf_op | source)
XLA Modules:
  0.0 270.7 jit_solution(8040783505415680214)
XLA Ops:
  6.5 0.0 all-gather.3.cloned.1.call-start
  6.5 0.8 copy.20
  7.3 8.7 %collective-permute-start.1 = (bf16[32,1,128]{2,0,1:T(8,128)(2,1)S(1)}, bf16[32,1,128]{2,0,1:T(8,128)(2,1)S(1)}, u32[]{:S(2)}, u32[]{:S(2)}) collective-permute-start(bf16[32,1,128]{2,0,1:T(8,128)(2,1)S(1)} %get-tuple-element.6), channel_id=1, source_target_pairs={{32,0},{64,32},{96,64},{128,96},{160,128},{192,160},{224,192},{256... | collective-permute-start | bytes 24584 | tf_op jit(solution)/shard_map/ppermute | solution.py:18
  16.1 1.9 collective-permute-start
  18.0 0.0 collective-permute-done.1
  18.0 1.1 collective-permute-done
  19.1 0.6 pad_maximum_fusion
  19.8 0.0 all-gather.3.cloned.1.call-update
  19.8 0.0 all-gather.5.cloned.1.call-start
  19.8 2.4 copy.27
  22.3 0.0 all-gather.5.cloned.1.call-update
  22.3 111.9 %all-gather.3.cloned.1.call-done = bf16[1024,6,128]{2,0,1:T(8,128)(2,1)} async-done(((bf16[32,6,128]{2,0,1:T(8,128)(2,1)}), bf16[1024,6,128]{2,0,1:T(8,128)(2,1)}) %all-gather.3.cloned.1.call-update) | async-done | bytes 1572880 | tf_op jit(solution)/shard_map/all_gather | solution.py:44
  134.2 1.7 copy.23
  135.9 1.2 copy.32
  137.1 0.8 pad.clone
  138.0 0.6 copy.26
  138.6 0.2 slice.12
  138.8 0.0 copy-start.1
  138.8 102.8 %all-gather.5.cloned.1.call-done = bf16[27,32,1024]{1,0,2:T(8,128)(2,1)} async-done(((bf16[27,32,64]{1,0,2:T(8,128)(2,1)}), bf16[27,32,1024]{1,0,2:T(8,128)(2,1)}) %all-gather.5.cloned.1.call-update) | async-done | bytes 1769488 | tf_op jit(solution)/shard_map/all_gather | solution.py:40
  241.6 10.3 %copy.28 = bf16[27,32,1024]{2,1,0:T(8,128)(2,1)} copy(bf16[27,32,1024]{1,0,2:T(8,128)(2,1)} %all-gather.5.cloned.1.call-done) | data formatting | bytes 3538944 | tf_op jit(solution)/shard_map/all_gather | solution.py:40
  251.9 0.0 copy-done.1
  251.9 0.0 copy-start
  251.9 10.7 %fusion.9 = f32[4,4,8,5,32]{4,2,3,1,0:T(8,128)S(1)} fusion(bf16[3,3,3,32,1024]{4,3,2,1,0:T(8,128)(2,1)} %bitcast.16, bf16[1024,6,4,1,7,2]{0,4,5,2,1,3:T(8,128)(2,1)S(1)} %slice.12, bf16[1024,6,4,1,8,5]{0,4,5,2,1,3:T(8,128)(2,1)S(1)} %copy.26, pred[8,5]{0,1:T(8,128)(4,1)S(1)} %copy-done.1), kind=kOutput, calls=%fused_computation.9 | convolution fusion | flops 951996416 | bytes 4505640 | tf_op jit(solution)/shard_map/conv_general_dilated | solution.py:28
  262.6 0.1 copy.29
  262.8 0.2 copy.30
  262.9 0.2 reshape_squeeze.3
  263.1 0.0 copy-done
  263.1 0.1 add_convert_fusion
  263.2 0.6 copy.31
  (2 shorter events, 0.0 us)
Async XLA Ops:
  6.5 127.6 %all-gather.3.cloned.1.call-start = ((), (), s32[]{:S(2)}) async-start(), calls=%async_computation | async-start | bytes 1622016 | tf_op jit(solution)/shard_map/all_gather | solution.py:44
  7.3 10.7 %collective-permute-start.1 = (bf16[32,1,128]{2,0,1:T(8,128)(2,1)S(1)}, bf16[32,1,128]{2,0,1:T(8,128)(2,1)S(1)}, u32[]{:S(2)}, u32[]{:S(2)}) collective-permute-start(bf16[32,1,128]{2,0,1:T(8,128)(2,1)S(1)} %get-tuple-element.6), channel_id=1, source_target_pairs={{32,0},{64,32},{96,64},{128,96},{160,128},{192,160},{224,192},{256... | collective-permute-start | bytes 24584 | tf_op jit(solution)/shard_map/ppermute | solution.py:18
  16.1 3.1 %collective-permute-start = (bf16[32,1,128]{2,0,1:T(8,128)(2,1)S(1)}, bf16[32,1,128]{2,0,1:T(8,128)(2,1)S(1)}, u32[]{:S(2)}, u32[]{:S(2)}) collective-permute-start(bf16[32,1,128]{2,0,1:T(8,128)(2,1)S(1)} %get-tuple-element.5), channel_id=1, source_target_pairs={{0,32},{32,64},{64,96},{96,128},{128,160},{160,192},{192,224},{224... | collective-permute-start | bytes 24584 | tf_op jit(solution)/shard_map/ppermute | solution.py:15
  19.8 221.8 %all-gather.5.cloned.1.call-start = ((), (), s32[]{:S(2)}) async-start(), calls=%async_computation.1 | async-start | bytes 8912896 | tf_op jit(solution)/shard_map/all_gather | solution.py:40
  138.8 113.1 %copy-start.1 = (pred[8,5]{0,1:T(8,128)(4,1)S(1)}, pred[8,5]{0,1:T(8,128)(4,1)}, u32[]{:S(2)}) copy-start(pred[8,5]{0,1:T(8,128)(4,1)} %constant.5) | copy-start | bytes 124
  251.9 11.2 %copy-start = (f32[32]{0:T(128)S(1)}, f32[32]{0:T(128)}, u32[]{:S(2)}) copy-start(f32[32]{0:T(128)} %param.5) | copy-start | bytes 388
Sparse Core Ops, SparseCore 0:
  19.9 114.2 all-gather.2
  137.5 104.0 all-gather.4
where the time goes:
time: 271 us
  waiting for transfers between devices  216 us (80%)
  local copies, waits for them, and re-layouts  19.2 us (7%)
  between operations  13.5 us (5%)
  starting transfers between devices  10.7 us (4%)
  matrix products  10.7 us (4%)
    all_gather x1, waiting for transfers between devices, shards(): whole_rimmed = lax.all_gather(rimmed, 'filt', axis=0, tiled=True)  112 us
    all_gather x1, waiting for transfers between devices, shards(): gathered = lax.all_gather(kernel, 'vox', axis=2, tiled=True)  103 us
    conv_general_dilated x1, matrix products, convolve(): lax.conv_general_dilated(shaped, weights, (1, 1, 1), [(0, 0), (1, 1), (1,...  10.7 us
    all_gather x1, local copies, waits for them, and re-layouts, shards(): gathered = lax.all_gather(kernel, 'vox', axis=2, tiled=True)  10.3 us
    ppermute x1, starting transfers between devices, padded(): lax.ppermute(lax.slice_in_dim(block, 0, width, axis=dim), axis, backward)  8.75 us
  transfers between devices with their start and end apart: 4, of which 3 were waited for; matrix products, arithmetic and copies ran while one was open for 3% of the time, Pallas kernels for 0%

commit v1 on v0

v1 whole, which is shorter than its diff:
```python
import jax
import jax.numpy as jnp
from jax import lax
from jax.experimental import pallas as pl
from jax.experimental.pallas import tpu as pltpu
from jax.sharding import Mesh, PartitionSpec as P


AXES = ("xh", "y", "core", "xl", "z")
LANES = 128
TAPS = 27
FILT = 32
ROWS = TAPS * FILT
HALF = ROWS // 2


def pack_kernel(w_ref, o_ref):
    w = w_ref[...].reshape(ROWS, 64)
    o_ref[...] = jnp.concatenate([w[:HALF], w[HALF:]], axis=1)


def pack(kernel):
    return pl.pallas_call(
        pack_kernel,
        out_shape=jax.ShapeDtypeStruct((HALF, LANES), jnp.bfloat16),
        in_specs=[pl.BlockSpec(memory_space=pltpu.VMEM)],
        out_specs=pl.BlockSpec(memory_space=pltpu.VMEM),
        name="pack",
    )(kernel)


def conv_kernel(s_ref, own_ref, pair_ref, x_ref, lo_ref, hi_ref, o_ref, xs, zs):
    swap = s_ref[0]
    y = s_ref[1]
    core = s_ref[2]
    for dy in range(4):
        q = lax.rem(y + dy, 4)
        for part in range(2):
            rows = slice(dy * 128 + part * 64, dy * 128 + part * 64 + 64)
            z = pl.ds(4 * q + 2 * (core ^ part), 2)
            xs[rows, 0:128] = lo_ref[z].reshape(64, LANES)
            xs[rows, 640:768] = hi_ref[z].reshape(64, LANES)
            for d in range(4):
                xs[rows, (d + 1) * 128 : (d + 2) * 128] = x_ref[z, d].reshape(64, LANES)
    lane = lax.broadcasted_iota(jnp.int32, (FILT, LANES), 1)
    row, cell = lane // 32, lane % 32
    for r in range(2):
        first = []
        second = []
        for dy in range(4):
            a = own_ref[4 * r + dy]
            b = pair_ref[4 * r + dy]
            first.append(jnp.concatenate([a[:, :64], b[:, :64]], axis=1))
            second.append(jnp.concatenate([a[:, 64:], b[:, 64:]], axis=1))
        zs[0:HALF] = jnp.dot(jnp.concatenate(first, axis=1), xs[...], preferred_element_type=jnp.float32)
        zs[HALF:ROWS] = jnp.dot(jnp.concatenate(second, axis=1), xs[...], preferred_element_type=jnp.float32)
        for d in range(4):
            total = None
            for b in range(3):
                for e in range(3):
                    part = None
                    for a in range(3):
                        tap = 9 * a + 3 * b + e
                        piece = zs[tap * FILT : (tap + 1) * FILT, (d + a) * 128 : (d + a + 1) * 128]
                        part = piece if part is None else part + piece
                    shift = (b - 1) * 32 + (e - 1)
                    if shift != 0:
                        part = pltpu.roll(part, (-shift) % LANES, 1)
                        ok = (row + (b - 1) >= 0) & (row + (b - 1) < 4) & (cell + (e - 1) >= 0) & (cell + (e - 1) < 32)
                        part = jnp.where(ok, part, 0.0)
                    total = part if total is None else total + part
            o_ref[r ^ swap, d] = total


def conv(scalars, own, pair, x, lo, hi):
    vm = pl.BlockSpec(memory_space=pltpu.VMEM)
    return pl.pallas_call(
        conv_kernel,
        out_shape=jax.ShapeDtypeStruct((2, 4, FILT, LANES), jnp.float32),
        in_specs=[pl.BlockSpec(memory_space=pltpu.SMEM), vm, vm, vm, vm, vm],
        out_specs=vm,
        scratch_shapes=[pltpu.VMEM((512, 768), jnp.bfloat16), pltpu.VMEM((ROWS, 768), jnp.float32)],
        name="conv",
    )(scalars, own, pair, x, lo, hi)


def flat(xh, y, xl):
    return (xh * 4 + y) * 2 + xl


def work(volume, kernel, bias):
    xh = lax.axis_index("xh")
    xl = lax.axis_index("xl")
    y = lax.axis_index("y")
    x = volume.transpose(1, 0, 2)
    spread = jnp.broadcast_to(x[None], (16,) + x.shape)
    x_all = lax.all_to_all(spread, "z", 0, 0, tiled=True)
    packed = pack(kernel)
    pieces = []
    for r in range(2):
        for dy in range(4):
            pairs = [
                (flat(tl, (ty + dy) % 4, (th + r) % 2), flat(th, ty, tl))
                for th in range(2)
                for ty in range(4)
                for tl in range(2)
            ]
            pieces.append(lax.ppermute(packed, ("xh", "y", "xl"), pairs))
    own = jnp.stack(pieces)
    pair = lax.ppermute(own, "core", [(0, 1), (1, 0)])
    up = [(i, i + 1) for i in range(15)]
    down = [(i + 1, i) for i in range(15)]
    lo = lax.ppermute(x_all[:, 3], ("xh", "y", "core"), up)
    hi = lax.ppermute(x_all[:, 0], ("xh", "y", "core"), down)
    scalars = jnp.stack([jnp.bitwise_xor(xh, xl), y, lax.axis_index("core")]).astype(jnp.int32)
    partial = conv(scalars, own, pair, x_all, lo, hi)
    other = lax.ppermute(partial[1], "xl", [(0, 1), (1, 0)])
    out = partial[0] + other + bias[None, :, None]
    return out.astype(jnp.bfloat16).transpose(1, 0, 2)


def solution(mesh):
    fine = Mesh(mesh.devices.reshape(2, 4, 2, 2, 16), AXES)
    vox = ("xh", "y", "core")
    filt = ("xl", "z")
    in_specs = (P(filt, vox, None), P(None, filt, vox), P(filt))
    return jax.shard_map(work, mesh=fine, in_specs=in_specs, out_specs=P(filt, vox, None), check_vma=False)
```

time: 271 us -> 88.2 us (0.33)
  the two profiles are of different devices: /device:TPU:1 before, /device:TPU:38 now
where the time goes in v1:
time: 88.2 us; the launch traced here: 87.6 us
  starting transfers between devices  53.5 us (61%)
  waiting for transfers between devices  24.1 us (27%)
  Pallas kernels  5.74 us (7%)
  local copies, waits for them, and re-layouts  3.3 us (4%)
    ppermute x8, starting transfers between devices, work(): pieces.append(lax.ppermute(packed, ('xh', 'y', 'xl'), pairs))  30 us
    all_to_all x1, starting transfers between devices, work(): x_all = lax.all_to_all(spread, 'z', 0, 0, tiled=True)  15.3 us
    ppermute x1, waiting for transfers between devices, work(): lo = lax.ppermute(x_all[:, 3], ('xh', 'y', 'core'), up)  6.86 us
    ppermute x8, waiting for transfers between devices, work(): pieces.append(lax.ppermute(packed, ('xh', 'y', 'xl'), pairs))  6.69 us
    all_to_all x1, waiting for transfers between devices, work(): x_all = lax.all_to_all(spread, 'z', 0, 0, tiled=True)  6.31 us
    ppermute x1, waiting for transfers between devices, work(): other = lax.ppermute(partial[1], 'xl', [(0, 1), (1, 0)])  4.23 us
    pallas_call x1, Pallas kernels, conv(): pl.pallas_call(conv_kernel, out_shape=jax.ShapeDtypeStruct((2, 4, FILT, L...  4.06 us
    ppermute x1, starting transfers between devices, work(): lo = lax.ppermute(x_all[:, 3], ('xh', 'y', 'core'), up)  2.41 us
  transfers between devices with their start and end apart: 13, of which 5 were waited for; matrix products, arithmetic and copies ran while one was open for 2% of the time, Pallas kernels for 0%

profile of v1, /device:TPU:38, one launch (start us, length us, event | category | flops | bytes accessed | tf_op | source)
XLA Modules:
  0.0 87.6 jit_solution(15362649330958419597)
XLA Ops:
  0.0 0.0 copy-start.7
  0.0 1.7 %pack.1 = bf16[432,128]{1,0:T(8,128)(2,1)} custom-call(bf16[27,32,64]{2,1,0:T(8,128)(2,1)} %w_ref.1), custom_call_target="tpu_custom_call" | custom-call | tf_op jit(solution)/shard_map/pack/pallas_call | solution.py:23
  1.7 1.5 %collective-permute-start = (bf16[432,128]{1,0:T(8,128)(2,1)}, bf16[432,128]{1,0:T(8,128)(2,1)S(1)}, u32[]{:S(2)}, u32[]{:S(2)}) collective-permute-start(bf16[432,128]{1,0:T(8,128)(2,1)} %pack.1), channel_id=1, source_target_pairs={{0,0},{256,16},{64,64},{320,80},{128,128},{384,144},{192,192},{448... | collective-permute-start | bytes 331784 | tf_op jit(solution)/shard_map/ppermute | solution.py:108
  3.2 4.9 %collective-permute-start.1 = (bf16[432,128]{1,0:T(8,128)(2,1)}, bf16[432,128]{1,0:T(8,128)(2,1)S(1)}, u32[]{:S(2)}, u32[]{:S(2)}) collective-permute-start(bf16[432,128]{1,0:T(8,128)(2,1)} %pack.1), channel_id=1, source_target_pairs={{64,0},{320,16},{128,64},{384,80},{192,128},{448,144},{0,192},{256... | collective-permute-start | bytes 331784 | tf_op jit(solution)/shard_map/ppermute | solution.py:108
  8.1 2.5 %collective-permute-start.2 = (bf16[432,128]{1,0:T(8,128)(2,1)}, bf16[432,128]{1,0:T(8,128)(2,1)S(1)}, u32[]{:S(2)}, u32[]{:S(2)}) collective-permute-start(bf16[432,128]{1,0:T(8,128)(2,1)} %pack.1), channel_id=1, source_target_pairs={{128,0},{384,16},{192,64},{448,80},{0,128},{256,144},{64,192},{320... | collective-permute-start | bytes 331784 | tf_op jit(solution)/shard_map/ppermute | solution.py:108
  10.7 2.9 %collective-permute-start.3 = (bf16[432,128]{1,0:T(8,128)(2,1)}, bf16[432,128]{1,0:T(8,128)(2,1)S(1)}, u32[]{:S(2)}, u32[]{:S(2)}) collective-permute-start(bf16[432,128]{1,0:T(8,128)(2,1)} %pack.1), channel_id=1, source_target_pairs={{192,0},{448,16},{0,64},{256,80},{64,128},{320,144},{128,192},{384... | collective-permute-start | bytes 331784 | tf_op jit(solution)/shard_map/ppermute | solution.py:108
  13.6 6.0 %collective-permute-start.4 = (bf16[432,128]{1,0:T(8,128)(2,1)}, bf16[432,128]{1,0:T(8,128)(2,1)S(1)}, u32[]{:S(2)}, u32[]{:S(2)}) collective-permute-start(bf16[432,128]{1,0:T(8,128)(2,1)} %pack.1), channel_id=1, source_target_pairs={{16,0},{272,16},{80,64},{336,80},{144,128},{400,144},{208,192},{46... | collective-permute-start | bytes 331784 | tf_op jit(solution)/shard_map/ppermute | solution.py:108
  19.6 0.0 copy-done.7
  19.6 0.9 %broadcast_in_dim.2 = bf16[16,4,32,128]{3,2,1,0:T(8,128)(2,1)} broadcast(bf16[4,32,128]{2,1,0:T(8,128)(2,1)S(1)} %copy.7), dimensions={1,2,3} | broadcast | bytes 557056 | tf_op jit(solution)/shard_map/broadcast_in_dim | solution.py:96
  20.6 0.0 copy-start.6
  20.6 15.3 %all-to-all-start = ((bf16[16,4,32,128]{3,2,1,0:T(8,128)(2,1)}), bf16[16,4,32,128]{3,2,1,0:T(8,128)(2,1)S(1)}, u32[]{:S(2)}, u32[]{:S(2)}) async-start(bf16[16,4,32,128]{3,2,1,0:T(8,128)(2,1)} %broadcast_in_dim.2), calls=%async_computation | async-start | bytes 1048576 | tf_op jit(solution)/shard_map/all_to_all | solution.py:97
  35.9 0.0 collective-permute-done
  35.9 0.0 copy-done.6
  35.9 3.6 %collective-permute-start.5 = (bf16[432,128]{1,0:T(8,128)(2,1)S(1)}, bf16[432,128]{1,0:T(8,128)(2,1)S(1)}, u32[]{:S(2)}, u32[]{:S(2)}) collective-permute-start(bf16[432,128]{1,0:T(8,128)(2,1)S(1)} %copy-done.6), channel_id=1, source_target_pairs={{80,0},{336,16},{144,64},{400,80},{208,128},{464,144},{16,192},{27... | collective-permute-start | bytes 331784 | tf_op jit(solution)/shard_map/ppermute | solution.py:108
  39.6 0.0 collective-permute-done.1
  39.6 6.6 %collective-permute-start.6 = (bf16[432,128]{1,0:T(8,128)(2,1)S(1)}, bf16[432,128]{1,0:T(8,128)(2,1)S(1)}, u32[]{:S(2)}, u32[]{:S(2)}) collective-permute-start(bf16[432,128]{1,0:T(8,128)(2,1)S(1)} %copy-done.6), channel_id=1, source_target_pairs={{144,0},{400,16},{208,64},{464,80},{16,128},{272,144},{80,192},{33... | collective-permute-start | bytes 331784 | tf_op jit(solution)/shard_map/ppermute | solution.py:108
  46.2 0.0 collective-permute-done.2
  46.2 1.9 %collective-permute-start.7 = (bf16[432,128]{1,0:T(8,128)(2,1)S(1)}, bf16[432,128]{1,0:T(8,128)(2,1)S(1)}, u32[]{:S(2)}, u32[]{:S(2)}) collective-permute-start(bf16[432,128]{1,0:T(8,128)(2,1)S(1)} %copy-done.6), channel_id=1, source_target_pairs={{208,0},{464,16},{16,64},{272,80},{80,128},{336,144},{144,192},{40... | collective-permute-start | bytes 331784 | tf_op jit(solution)/shard_map/ppermute | solution.py:108
  48.2 0.0 collective-permute-done.3
  48.2 0.0 collective-permute-done.4
  48.2 0.0 collective-permute-done.5
  48.3 0.4 collective-permute-done.6
  48.7 6.3 %collective-permute-done.7 = bf16[432,128]{1,0:T(8,128)(2,1)S(1)} collective-permute-done((bf16[432,128]{1,0:T(8,128)(2,1)S(1)}, bf16[432,128]{1,0:T(8,128)(2,1)S(1)}, u32[]{:S(2)}, u32[]{:S(2)}) %collective-permute-start.7) | collective-permute-done | bytes 110624 | tf_op jit(solution)/shard_map/ppermute | solution.py:108
  55.0 0.0 copy-start.1
  55.0 1.9 %collective-permute-start.8 = (bf16[8,432,128]{2,1,0:T(8,128)(2,1)S(1)}, bf16[8,432,128]{2,1,0:T(8,128)(2,1)S(1)}, u32[]{:S(2)}, u32[]{:S(2)}) collective-permute-start(bf16[8,432,128]{2,1,0:T(8,128)(2,1)S(1)} %bitcast_dynamic-update-slice_fusion.own_ref), channel_id=1, source_target_pairs={{0,32},{32,0},{1,33},{33,1},{2,34},{34,2},{3,35},{35,3},{4,36},{36... | collective-permute-start | bytes 2654216 | tf_op jit(solution)/shard_map/ppermute | solution.py:110
  56.9 6.3 %all-to-all-done.x_ref = bf16[16,4,32,128]{3,2,1,0:T(8,128)(2,1)S(1)} async-done(((bf16[16,4,32,128]{3,2,1,0:T(8,128)(2,1)}), bf16[16,4,32,128]{3,2,1,0:T(8,128)(2,1)S(1)}, u32[]{:S(2)}, u32[]{:S(2)}) %all-to-all-start) | async-done | bytes 524320 | tf_op jit(solution)/shard_map/all_to_all | solution.py:97
  63.2 0.0 copy-start
  63.3 1.9 %collective-permute-start.10 = (bf16[16,32,128]{2,1,0:T(8,128)(2,1)S(1)}, bf16[16,32,128]{2,1,0:T(8,128)(2,1)S(1)}, u32[]{:S(2)}, u32[]{:S(2)}) collective-permute-start(bf16[16,32,128]{2,1,0:T(8,128)(2,1)S(1)} %get-tuple-element.5), channel_id=1, source_target_pairs={{32,0},{64,32},{96,64},{128,96},{160,128},{192,160},{224,192},{256... | collective-permute-start | bytes 393224 | tf_op jit(solution)/shard_map/ppermute | solution.py:114
  65.2 2.4 %collective-permute-start.9 = (bf16[16,32,128]{2,1,0:T(8,128)(2,1)S(1)}, bf16[16,32,128]{2,1,0:T(8,128)(2,1)S(1)}, u32[]{:S(2)}, u32[]{:S(2)}) collective-permute-start(bf16[16,32,128]{2,1,0:T(8,128)(2,1)S(1)} %get-tuple-element.6), channel_id=1, source_target_pairs={{0,32},{32,64},{64,96},{96,128},{128,160},{160,192},{192,224},{224... | collective-permute-start | bytes 393224 | tf_op jit(solution)/shard_map/ppermute | solution.py:113
  67.6 0.6 pad_add_fusion.s_ref
  68.2 0.0 collective-permute-done.8.pair_ref
  68.2 0.0 copy-start.2
  68.2 0.0 collective-permute-done.10.hi_ref
  68.2 0.0 copy-start.4
  68.2 6.9 %collective-permute-done.9.lo_ref = bf16[16,32,128]{2,1,0:T(8,128)(2,1)S(1)} collective-permute-done((bf16[16,32,128]{2,1,0:T(8,128)(2,1)S(1)}, bf16[16,32,128]{2,1,0:T(8,128)(2,1)S(1)}, u32[]{:S(2)}, u32[]{:S(2)}) %collective-permute-start.9) | collective-permute-done | bytes 131104 | tf_op jit(solution)/shard_map/ppermute | solution.py:113
  75.1 0.0 copy-done.1
  75.1 0.0 copy-done
  75.1 0.0 copy-done.2
  75.1 0.0 copy-done.4
  75.1 0.0 copy-start.5
  75.1 0.6 copy-done.5
  75.8 0.0 copy-start.8
  75.8 4.1 %conv.1 = f32[2,4,32,128]{3,2,1,0:T(8,128)} custom-call(s32[3]{0:T(128)} %pad_add_fusion.s_ref, bf16[8,432,128]{2,1,0:T(8,128)(2,1)} %copy-done.1, bf16[8,432,128]{2,1,0:T(8,128)(2,1)} %copy-done.2, bf16[16,4,32,128]{3,2,1,0:T(8,128)(2,1)} %copy-done, bf16[16,32,128]{2,1,0:T(8,128)(2,1)} %copy-done.5, bf16[16,32,128]{2,1,0:T(8,128)(2,1)} %copy-done.4), custom_call_target="tpu_custom_call" | custom-call | tf_op jit(solution)/shard_map/conv/pallas_call | solution.py:77
  79.8 0.0 copy-start.3
  79.8 0.9 %slice_bitcast_fusion.2 = f32[4,32,128]{2,1,0:T(8,128)S(1)} fusion(f32[2,4,32,128]{3,2,1,0:T(8,128)} %conv.1), kind=kLoop, calls=%fused_computation.10 | loop fusion | bytes 131072 | tf_op jit(solution)/shard_map/squeeze | solution.py:117
  80.8 1.9 %collective-permute-start.11 = (f32[4,32,128]{2,1,0:T(8,128)S(1)}, f32[4,32,128]{2,1,0:T(8,128)S(1)}, u32[]{:S(2)}, u32[]{:S(2)}) collective-permute-start(f32[4,32,128]{2,1,0:T(8,128)S(1)} %slice_bitcast_fusion.2), channel_id=1, source_target_pairs={{0,16},{16,0},{1,17},{17,1},{2,18},{18,2},{3,19},{19,3},{4,20},{20... | collective-permute-start | bytes 196616 | tf_op jit(solution)/shard_map/ppermute | solution.py:117
  82.7 4.2 %collective-permute-done.11 = f32[4,32,128]{2,1,0:T(8,128)S(1)} collective-permute-done((f32[4,32,128]{2,1,0:T(8,128)S(1)}, f32[4,32,128]{2,1,0:T(8,128)S(1)}, u32[]{:S(2)}, u32[]{:S(2)}) %collective-permute-start.11) | collective-permute-done | bytes 65568 | tf_op jit(solution)/shard_map/ppermute | solution.py:117
  86.9 0.0 copy-done.8
  86.9 0.0 copy-done.3
  86.9 0.1 fusion.3
  87.0 0.6 copy.10
  (10 shorter events, 0.1 us)
Async XLA Ops:
  0.0 19.6 %copy-start.7 = (bf16[32,4,128]{2,1,0:T(4,128)(2,1)S(1)}, bf16[32,4,128]{2,1,0:T(4,128)(2,1)}, u32[]{:S(2)}) copy-start(bf16[32,4,128]{2,1,0:T(4,128)(2,1)} %param.3) | copy-start | bytes 98308
  1.7 34.3 %collective-permute-start = (bf16[432,128]{1,0:T(8,128)(2,1)}, bf16[432,128]{1,0:T(8,128)(2,1)S(1)}, u32[]{:S(2)}, u32[]{:S(2)}) collective-permute-start(bf16[432,128]{1,0:T(8,128)(2,1)} %pack.1), channel_id=1, source_target_pairs={{0,0},{256,16},{64,64},{320,80},{128,128},{384,144},{192,192},{448... | collective-permute-start | bytes 331784 | tf_op jit(solution)/shard_map/ppermute | solution.py:108
  3.2 36.4 %collective-permute-start.1 = (bf16[432,128]{1,0:T(8,128)(2,1)}, bf16[432,128]{1,0:T(8,128)(2,1)S(1)}, u32[]{:S(2)}, u32[]{:S(2)}) collective-permute-start(bf16[432,128]{1,0:T(8,128)(2,1)} %pack.1), channel_id=1, source_target_pairs={{64,0},{320,16},{128,64},{384,80},{192,128},{448,144},{0,192},{256... | collective-permute-start | bytes 331784 | tf_op jit(solution)/shard_map/ppermute | solution.py:108
  8.1 38.1 %collective-permute-start.2 = (bf16[432,128]{1,0:T(8,128)(2,1)}, bf16[432,128]{1,0:T(8,128)(2,1)S(1)}, u32[]{:S(2)}, u32[]{:S(2)}) collective-permute-start(bf16[432,128]{1,0:T(8,128)(2,1)} %pack.1), channel_id=1, source_target_pairs={{128,0},{384,16},{192,64},{448,80},{0,128},{256,144},{64,192},{320... | collective-permute-start | bytes 331784 | tf_op jit(solution)/shard_map/ppermute | solution.py:108
  10.7 37.5 %collective-permute-start.3 = (bf16[432,128]{1,0:T(8,128)(2,1)}, bf16[432,128]{1,0:T(8,128)(2,1)S(1)}, u32[]{:S(2)}, u32[]{:S(2)}) collective-permute-start(bf16[432,128]{1,0:T(8,128)(2,1)} %pack.1), channel_id=1, source_target_pairs={{192,0},{448,16},{0,64},{256,80},{64,128},{320,144},{128,192},{384... | collective-permute-start | bytes 331784 | tf_op jit(solution)/shard_map/ppermute | solution.py:108
  13.6 34.6 %collective-permute-start.4 = (bf16[432,128]{1,0:T(8,128)(2,1)}, bf16[432,128]{1,0:T(8,128)(2,1)S(1)}, u32[]{:S(2)}, u32[]{:S(2)}) collective-permute-start(bf16[432,128]{1,0:T(8,128)(2,1)} %pack.1), channel_id=1, source_target_pairs={{16,0},{272,16},{80,64},{336,80},{144,128},{400,144},{208,192},{46... | collective-permute-start | bytes 331784 | tf_op jit(solution)/shard_map/ppermute | solution.py:108
  20.6 15.4 %copy-start.6 = (bf16[432,128]{1,0:T(8,128)(2,1)S(1)}, bf16[432,128]{1,0:T(8,128)(2,1)}, u32[]{:S(2)}) copy-start(bf16[432,128]{1,0:T(8,128)(2,1)} %pack.1) | copy-start | bytes 331780
  20.6 42.7 %all-to-all-start = ((bf16[16,4,32,128]{3,2,1,0:T(8,128)(2,1)}), bf16[16,4,32,128]{3,2,1,0:T(8,128)(2,1)S(1)}, u32[]{:S(2)}, u32[]{:S(2)}) async-start(bf16[16,4,32,128]{3,2,1,0:T(8,128)(2,1)} %broadcast_in_dim.2), calls=%async_computation | async-start | bytes 1048576 | tf_op jit(solution)/shard_map/all_to_all | solution.py:97
  35.9 12.3 %collective-permute-start.5 = (bf16[432,128]{1,0:T(8,128)(2,1)S(1)}, bf16[432,128]{1,0:T(8,128)(2,1)S(1)}, u32[]{:S(2)}, u32[]{:S(2)}) collective-permute-start(bf16[432,128]{1,0:T(8,128)(2,1)S(1)} %copy-done.6), channel_id=1, source_target_pairs={{80,0},{336,16},{144,64},{400,80},{208,128},{464,144},{16,192},{27... | collective-permute-start | bytes 331784 | tf_op jit(solution)/shard_map/ppermute | solution.py:108
  39.6 9.0 %collective-permute-start.6 = (bf16[432,128]{1,0:T(8,128)(2,1)S(1)}, bf16[432,128]{1,0:T(8,128)(2,1)S(1)}, u32[]{:S(2)}, u32[]{:S(2)}) collective-permute-start(bf16[432,128]{1,0:T(8,128)(2,1)S(1)} %copy-done.6), channel_id=1, source_target_pairs={{144,0},{400,16},{208,64},{464,80},{16,128},{272,144},{80,192},{33... | collective-permute-start | bytes 331784 | tf_op jit(solution)/shard_map/ppermute | solution.py:108
  46.2 8.8 %collective-permute-start.7 = (bf16[432,128]{1,0:T(8,128)(2,1)S(1)}, bf16[432,128]{1,0:T(8,128)(2,1)S(1)}, u32[]{:S(2)}, u32[]{:S(2)}) collective-permute-start(bf16[432,128]{1,0:T(8,128)(2,1)S(1)} %copy-done.6), channel_id=1, source_target_pairs={{208,0},{464,16},{16,64},{272,80},{80,128},{336,144},{144,192},{40... | collective-permute-start | bytes 331784 | tf_op jit(solution)/shard_map/ppermute | solution.py:108
  55.0 20.1 %copy-start.1 = (bf16[8,432,128]{2,1,0:T(8,128)(2,1)}, bf16[8,432,128]{2,1,0:T(8,128)(2,1)S(1)}, u32[]{:S(2)}) copy-start(bf16[8,432,128]{2,1,0:T(8,128)(2,1)S(1)} %bitcast_dynamic-update-slice_fusion.own_ref) | copy-start | bytes 2654212
  55.0 13.2 %collective-permute-start.8 = (bf16[8,432,128]{2,1,0:T(8,128)(2,1)S(1)}, bf16[8,432,128]{2,1,0:T(8,128)(2,1)S(1)}, u32[]{:S(2)}, u32[]{:S(2)}) collective-permute-start(bf16[8,432,128]{2,1,0:T(8,128)(2,1)S(1)} %bitcast_dynamic-update-slice_fusion.own_ref), channel_id=1, source_target_pairs={{0,32},{32,0},{1,33},{33,1},{2,34},{34,2},{3,35},{35,3},{4,36},{36... | collective-permute-start | bytes 2654216 | tf_op jit(solution)/shard_map/ppermute | solution.py:110
  63.2 11.9 %copy-start = (bf16[16,4,32,128]{3,2,1,0:T(8,128)(2,1)}, bf16[16,4,32,128]{3,2,1,0:T(8,128)(2,1)S(1)}, u32[]{:S(2)}) copy-start(bf16[16,4,32,128]{3,2,1,0:T(8,128)(2,1)S(1)} %all-to-all-done.x_ref) | copy-start | bytes 1572868
  63.3 5.0 %collective-permute-start.10 = (bf16[16,32,128]{2,1,0:T(8,128)(2,1)S(1)}, bf16[16,32,128]{2,1,0:T(8,128)(2,1)S(1)}, u32[]{:S(2)}, u32[]{:S(2)}) collective-permute-start(bf16[16,32,128]{2,1,0:T(8,128)(2,1)S(1)} %get-tuple-element.5), channel_id=1, source_target_pairs={{32,0},{64,32},{96,64},{128,96},{160,128},{192,160},{224,192},{256... | collective-permute-start | bytes 393224 | tf_op jit(solution)/shard_map/ppermute | solution.py:114
  65.2 9.9 %collective-permute-start.9 = (bf16[16,32,128]{2,1,0:T(8,128)(2,1)S(1)}, bf16[16,32,128]{2,1,0:T(8,128)(2,1)S(1)}, u32[]{:S(2)}, u32[]{:S(2)}) collective-permute-start(bf16[16,32,128]{2,1,0:T(8,128)(2,1)S(1)} %get-tuple-element.6), channel_id=1, source_target_pairs={{0,32},{32,64},{64,96},{96,128},{128,160},{160,192},{192,224},{224... | collective-permute-start | bytes 393224 | tf_op jit(solution)/shard_map/ppermute | solution.py:113
  68.2 6.9 %copy-start.2 = (bf16[8,432,128]{2,1,0:T(8,128)(2,1)}, bf16[8,432,128]{2,1,0:T(8,128)(2,1)S(1)}, u32[]{:S(2)}) copy-start(bf16[8,432,128]{2,1,0:T(8,128)(2,1)S(1)} %collective-permute-done.8.pair_ref) | copy-start | bytes 2654212
  68.2 6.9 %copy-start.4 = (bf16[16,32,128]{2,1,0:T(8,128)(2,1)}, bf16[16,32,128]{2,1,0:T(8,128)(2,1)S(1)}, u32[]{:S(2)}) copy-start(bf16[16,32,128]{2,1,0:T(8,128)(2,1)S(1)} %collective-permute-done.10.hi_ref) | copy-start | bytes 393220
  75.1 0.6 copy-start.5
  75.8 11.1 %copy-start.8 = (f32[32]{0:T(128)S(1)}, f32[32]{0:T(128)}, u32[]{:S(2)}) copy-start(f32[32]{0:T(128)} %param.5) | copy-start | bytes 388
  79.8 7.1 %copy-start.3 = (f32[2,4,32,128]{3,2,1,0:T(8,128)S(1)}, f32[2,4,32,128]{3,2,1,0:T(8,128)}, u32[]{:S(2)}) copy-start(f32[2,4,32,128]{3,2,1,0:T(8,128)} %conv.1) | copy-start | bytes 393220
  80.8 6.1 %collective-permute-start.11 = (f32[4,32,128]{2,1,0:T(8,128)S(1)}, f32[4,32,128]{2,1,0:T(8,128)S(1)}, u32[]{:S(2)}, u32[]{:S(2)}) collective-permute-start(f32[4,32,128]{2,1,0:T(8,128)S(1)} %slice_bitcast_fusion.2), channel_id=1, source_target_pairs={{0,16},{16,0},{1,17},{17,1},{2,18},{18,2},{3,19},{19,3},{4,20},{20... | collective-permute-start | bytes 196616 | tf_op jit(solution)/shard_map/ppermute | solution.py:117

commit v2 on v1

v2 whole, which is shorter than its diff:
```python
import jax
import jax.numpy as jnp
from jax import lax
from jax.experimental import pallas as pl
from jax.experimental.pallas import tpu as pltpu
from jax.sharding import Mesh, PartitionSpec as P


AXES = ("xh", "y", "core", "xl", "z")
LANES = 128
TAPS = 27
FILT = 32
ROWS = TAPS * FILT
HALF = ROWS // 2
VM = pl.BlockSpec(memory_space=pltpu.VMEM)


def spread_kernel(x_ref, o_ref):
    for d in range(4):
        plane = x_ref[:, d, :]
        for z in range(16):
            o_ref[z, d] = plane


def spread(volume):
    return pl.pallas_call(
        spread_kernel,
        out_shape=jax.ShapeDtypeStruct((16, 4, FILT, LANES), jnp.bfloat16),
        in_specs=[VM],
        out_specs=VM,
        name="spread",
    )(volume)


def pack_kernel(w_ref, o_ref):
    w = w_ref[...].reshape(ROWS, 64)
    o_ref[...] = jnp.concatenate([w[:HALF], w[HALF:]], axis=1)


def pack(kernel):
    return pl.pallas_call(
        pack_kernel,
        out_shape=jax.ShapeDtypeStruct((HALF, LANES), jnp.bfloat16),
        in_specs=[VM],
        out_specs=VM,
        name="pack",
    )(kernel)


def conv_kernel(flip, own_ref, pair_ref, x_ref, near_ref, far_ref, o_ref, xs, zs):
    core = lax.axis_index("core")
    group = lax.axis_index("xl") ^ lax.axis_index("xh") ^ flip
    for dy in range(4):
        q = dy
        for part in range(2):
            rows = slice(dy * 128 + part * 64, dy * 128 + part * 64 + 64)
            z = pl.ds(4 * q + 2 * (core ^ part), 2)
            xs[rows, pl.ds(pl.multiple_of(640 * (1 - core), 128), 128)] = near_ref[z].reshape(64, LANES)
            xs[rows, pl.ds(pl.multiple_of(640 * core, 128), 128)] = far_ref[z].reshape(64, LANES)
            for d in range(4):
                xs[rows, (d + 1) * 128 : (d + 2) * 128] = x_ref[z, d].reshape(64, LANES)
    lane = lax.broadcasted_iota(jnp.int32, (FILT, LANES), 1)
    row, cell = lane // 32, lane % 32
    first = []
    second = []
    for dy in range(4):
        a = own_ref[dy, group]
        b = pair_ref[dy, group]
        first.append(jnp.concatenate([a[:, :64], b[:, :64]], axis=1))
        second.append(jnp.concatenate([a[:, 64:], b[:, 64:]], axis=1))
    zs[0:HALF] = jnp.dot(jnp.concatenate(first, axis=1), xs[...], preferred_element_type=jnp.float32)
    zs[HALF:ROWS] = jnp.dot(jnp.concatenate(second, axis=1), xs[...], preferred_element_type=jnp.float32)
    for d in range(4):
        total = None
        for b in range(3):
            for e in range(3):
                part = None
                for a in range(3):
                    tap = 9 * a + 3 * b + e
                    piece = zs[tap * FILT : (tap + 1) * FILT, (d + a) * 128 : (d + a + 1) * 128]
                    part = piece if part is None else part + piece
                shift = (b - 1) * 32 + (e - 1)
                if shift != 0:
                    part = pltpu.roll(part, (-shift) % LANES, 1)
                    ok = (row + (b - 1) >= 0) & (row + (b - 1) < 4) & (cell + (e - 1) >= 0) & (cell + (e - 1) < 32)
                    part = jnp.where(ok, part, 0.0)
                total = part if total is None else total + part
        o_ref[d] = total


def conv(flip, own, pair, x, near, far):
    def body(*refs):
        conv_kernel(flip, *refs)

    return pl.pallas_call(
        body,
        out_shape=jax.ShapeDtypeStruct((4, FILT, LANES), jnp.float32),
        in_specs=[VM] * 5,
        out_specs=VM,
        scratch_shapes=[pltpu.VMEM((512, 768), jnp.bfloat16), pltpu.VMEM((ROWS, 768), jnp.float32)],
        name="conv_send" if flip else "conv_keep",
    )(own, pair, x, near, far)


def work(volume, kernel, bias):
    spread_x = spread(volume)
    x_all = lax.all_to_all(spread_x, "z", 0, 0, tiled=True)
    packed = pack(kernel)
    turned = []
    for r in range(2):
        pairs = [(2 * tl + (th + r) % 2, 2 * th + tl) for th in range(2) for tl in range(2)]
        turned.append(lax.ppermute(packed, ("xh", "xl"), pairs))
    both = jnp.stack(turned)
    own = lax.all_gather(both, "y", axis=0, tiled=False)
    pair = lax.ppermute(own, "core", [(0, 1), (1, 0)])
    core = lax.axis_index("core")
    outside = [(i, i - 1) if i % 2 == 0 else (i, i + 1) for i in range(1, 15)]
    near = lax.dynamic_index_in_dim(x_all, 3 * (1 - core), 1, keepdims=False)
    far = lax.dynamic_index_in_dim(x_all, 3 * core, 1, keepdims=False)
    far = lax.ppermute(far, ("xh", "y", "core"), outside)
    near = lax.ppermute(near, "core", [(0, 1), (1, 0)])
    own, pair, x_all, near, far = (pltpu.with_memory_space_constraint(v, pltpu.VMEM) for v in (own, pair, x_all, near, far))
    send = conv(1, own, pair, x_all, near, far)
    other = lax.ppermute(send, "xl", [(0, 1), (1, 0)])
    keep = conv(0, own, pair, x_all, near, far)
    return (keep + other + bias[None, :, None]).astype(jnp.bfloat16).transpose(1, 0, 2)


def solution(mesh):
    fine = Mesh(mesh.devices.reshape(2, 4, 2, 2, 16), AXES)
    vox = ("xh", "y", "core")
    filt = ("xl", "z")
    in_specs = (P(filt, vox, None), P(None, filt, vox), P(filt))
    return jax.shard_map(work, mesh=fine, in_specs=in_specs, out_specs=P(filt, vox, None), check_vma=False)
```

time: 88.2 us -> 66.2 us (0.75)
  the two profiles are of different devices: /device:TPU:38 before, /device:TPU:6 now
where the time goes in v2:
time: 66.2 us; the launch traced here: 65.7 us
  starting transfers between devices  31.9 us (48%)
  blocking collectives  14.3 us (22%)
  waiting for transfers between devices  10.9 us (16%)
  Pallas kernels  6.87 us (10%)
  other arithmetic  0.94 us (1%)
    all_to_all x1, starting transfers between devices, work(): x_all = lax.all_to_all(spread_x, 'z', 0, 0, tiled=True)  15.2 us
    all_gather x1, blocking collectives, work(): own = lax.all_gather(both, 'y', axis=0, tiled=False)  14.3 us
    ppermute x1, starting transfers between devices, work(): far = lax.ppermute(far, ('xh', 'y', 'core'), outside)  5.2 us
    ppermute x2, starting transfers between devices, work(): turned.append(lax.ppermute(packed, ('xh', 'xl'), pairs))  4.86 us
    all_to_all x1, waiting for transfers between devices, work(): x_all = lax.all_to_all(spread_x, 'z', 0, 0, tiled=True)  4.29 us
    pallas_call x2, Pallas kernels, conv(): pl.pallas_call(body, out_shape=jax.ShapeDtypeStruct((4, FILT, LANES), jnp...  3.47 us
    ppermute x1, starting transfers between devices, work(): other = lax.ppermute(send, 'xl', [(0, 1), (1, 0)])  2.84 us
    ppermute x1, waiting for transfers between devices, work(): far = lax.ppermute(far, ('xh', 'y', 'core'), outside)  2.75 us
  transfers between devices with their start and end apart: 7, of which 4 were waited for; matrix products, arithmetic and copies ran while one was open for 0% of the time, Pallas kernels for 5%

profile of v2, /device:TPU:6, one launch (start us, length us, event | category | flops | bytes accessed | tf_op | source)
XLA Modules:
  0.0 65.7 jit_solution(7131334867951166427)
XLA Ops:
  0.0 1.7 %spread.1 = bf16[16,4,32,128]{3,2,1,0:T(8,128)(2,1)} custom-call(bf16[32,4,128]{2,1,0:T(4,128)(2,1)} %x_ref.1), custom_call_target="tpu_custom_call" | custom-call | tf_op jit(solution)/shard_map/spread/pallas_call | solution.py:26
  1.7 15.2 %all-to-all-start = ((bf16[16,4,32,128]{3,2,1,0:T(8,128)(2,1)}), bf16[16,4,32,128]{3,2,1,0:T(8,128)(2,1)S(1)}, u32[]{:S(2)}, u32[]{:S(2)}) async-start(bf16[16,4,32,128]{3,2,1,0:T(8,128)(2,1)} %spread.1), calls=%async_computation | async-start | bytes 1048576 | tf_op jit(solution)/shard_map/all_to_all | solution.py:107
  16.9 1.7 %pack.1 = bf16[432,128]{1,0:T(8,128)(2,1)} custom-call(bf16[27,32,64]{2,1,0:T(8,128)(2,1)} %w_ref.1), custom_call_target="tpu_custom_call" | custom-call | tf_op jit(solution)/shard_map/pack/pallas_call | solution.py:41
  18.6 3.3 %collective-permute-start.1 = (bf16[432,128]{1,0:T(8,128)(2,1)}, bf16[432,128]{1,0:T(8,128)(2,1)S(1)}, u32[]{:S(2)}, u32[]{:S(2)}) collective-permute-start(bf16[432,128]{1,0:T(8,128)(2,1)} %pack.1), channel_id=1, source_target_pairs={{16,0},{272,16},{0,256},{256,272},{17,1},{273,17},{1,257},{257,273... | collective-permute-start | bytes 331784 | tf_op jit(solution)/shard_map/ppermute | solution.py:112
  21.9 1.6 %collective-permute-start = (bf16[432,128]{1,0:T(8,128)(2,1)}, bf16[432,128]{1,0:T(8,128)(2,1)S(1)}, u32[]{:S(2)}, u32[]{:S(2)}) collective-permute-start(bf16[432,128]{1,0:T(8,128)(2,1)} %pack.1), channel_id=1, source_target_pairs={{0,0},{256,16},{16,256},{272,272},{1,1},{257,17},{17,257},{273,273... | collective-permute-start | bytes 331784 | tf_op jit(solution)/shard_map/ppermute | solution.py:112
  23.5 2.0 %collective-permute-done.1 = bf16[432,128]{1,0:T(8,128)(2,1)S(1)} collective-permute-done((bf16[432,128]{1,0:T(8,128)(2,1)}, bf16[432,128]{1,0:T(8,128)(2,1)S(1)}, u32[]{:S(2)}, u32[]{:S(2)}) %collective-permute-start.1) | collective-permute-done | bytes 110624 | tf_op jit(solution)/shard_map/ppermute | solution.py:112
  25.4 0.0 collective-permute-done
  25.5 14.3 %all-gather = bf16[8,432,128]{2,1,0:T(8,128)(2,1)S(1)} all-gather(bf16[2,432,128]{2,1,0:T(8,128)(2,1)S(1)} %pad_maximum_fusion), channel_id=2, replica_groups=mesh['xh'=2,'y'=4,'core'=2,'xl'=2,'z'=16] {'y'}, dimensions={0}, use_global_device_ids=true | all-gather | bytes 1105920 | tf_op jit(solution)/shard_map/all_gather | solution.py:114
  39.8 1.9 %collective-permute-start.2 = (bf16[4,2,432,128]{3,2,1,0:T(8,128)(2,1)S(1)}, bf16[4,2,432,128]{3,2,1,0:T(8,128)(2,1)S(1)}, u32[]{:S(2)}, u32[]{:S(2)}) collective-permute-start(bf16[4,2,432,128]{3,2,1,0:T(8,128)(2,1)S(1)} %bitcast.9), channel_id=1, source_target_pairs={{0,32},{32,0},{1,33},{33,1},{2,34},{34,2},{3,35},{35,3},{4,36},{36... | collective-permute-start | bytes 2654216 | tf_op jit(solution)/shard_map/ppermute | solution.py:115
  41.7 4.3 %all-to-all-done.refs_2_ = bf16[16,4,32,128]{3,2,1,0:T(8,128)(2,1)S(1)} async-done(((bf16[16,4,32,128]{3,2,1,0:T(8,128)(2,1)}), bf16[16,4,32,128]{3,2,1,0:T(8,128)(2,1)S(1)}, u32[]{:S(2)}, u32[]{:S(2)}) %all-to-all-start) | async-done | bytes 524320 | tf_op jit(solution)/shard_map/all_to_all | solution.py:107
  46.0 5.2 %collective-permute-start.4 = (bf16[16,32,128]{2,1,0:T(8,128)(2,1)S(1)}, bf16[16,32,128]{2,1,0:T(8,128)(2,1)S(1)}, u32[]{:S(2)}, u32[]{:S(2)}) collective-permute-start(bf16[16,32,128]{2,1,0:T(8,128)(2,1)S(1)} %get-tuple-element.5), channel_id=1, source_target_pairs={{32,64},{64,32},{96,128},{128,96},{160,192},{192,160},{224,256},{2... | collective-permute-start | bytes 393224 | tf_op jit(solution)/shard_map/ppermute | solution.py:120
  51.2 1.9 %collective-permute-start.3 = (bf16[16,32,128]{2,1,0:T(8,128)(2,1)S(1)}, bf16[16,32,128]{2,1,0:T(8,128)(2,1)S(1)}, u32[]{:S(2)}, u32[]{:S(2)}) collective-permute-start(bf16[16,32,128]{2,1,0:T(8,128)(2,1)S(1)} %get-tuple-element.6), channel_id=1, source_target_pairs={{0,32},{32,0},{1,33},{33,1},{2,34},{34,2},{3,35},{35,3},{4,36},{36... | collective-permute-start | bytes 393224 | tf_op jit(solution)/shard_map/ppermute | solution.py:121
  53.2 0.0 collective-permute-done.2.refs_1_
  53.2 2.8 %collective-permute-done.4.refs_4_ = bf16[16,32,128]{2,1,0:T(8,128)(2,1)S(1)} collective-permute-done((bf16[16,32,128]{2,1,0:T(8,128)(2,1)S(1)}, bf16[16,32,128]{2,1,0:T(8,128)(2,1)S(1)}, u32[]{:S(2)}, u32[]{:S(2)}) %collective-permute-start.4) | collective-permute-done | bytes 131104 | tf_op jit(solution)/shard_map/ppermute | solution.py:120
  55.9 0.0 collective-permute-done.3.refs_3_
  55.9 1.7 %conv_send.1 = f32[4,32,128]{2,1,0:T(8,128)} custom-call(bf16[4,2,432,128]{3,2,1,0:T(8,128)(2,1)S(1)} %bitcast.10, bf16[4,2,432,128]{3,2,1,0:T(8,128)(2,1)S(1)} %collective-permute-done.2.refs_1_, bf16[16,4,32,128]{3,2,1,0:T(8,128)(2,1)S(1)} %all-to-all-done.refs_2_, bf16[16,32,128]{2,1,0:T(8,128)(2,1)S(1)} %collective-permute-done.3.refs_3_, ...), custom_call_target="tpu_custom_call" | custom-call | tf_op jit(solution)/shard_map/conv_send/pallas_call | solution.py:95
  57.7 0.0 copy-start
  57.7 2.8 %collective-permute-start.5 = (f32[4,32,128]{2,1,0:T(8,128)}, f32[4,32,128]{2,1,0:T(8,128)S(1)}, u32[]{:S(2)}, u32[]{:S(2)}) collective-permute-start(f32[4,32,128]{2,1,0:T(8,128)} %conv_send.1), channel_id=1, source_target_pairs={{0,16},{16,0},{1,17},{17,1},{2,18},{18,2},{3,19},{19,3},{4,20},{20... | collective-permute-start | bytes 196616 | tf_op jit(solution)/shard_map/ppermute | solution.py:124
  60.5 1.7 %conv_keep.1 = f32[4,32,128]{2,1,0:T(8,128)} custom-call(bf16[4,2,432,128]{3,2,1,0:T(8,128)(2,1)S(1)} %bitcast.11, bf16[4,2,432,128]{3,2,1,0:T(8,128)(2,1)S(1)} %collective-permute-done.2.refs_1_, bf16[16,4,32,128]{3,2,1,0:T(8,128)(2,1)S(1)} %all-to-all-done.refs_2_, bf16[16,32,128]{2,1,0:T(8,128)(2,1)S(1)} %collective-permute-done.3.refs_3_, ...), custom_call_target="tpu_custom_call" | custom-call | tf_op jit(solution)/shard_map/conv_keep/pallas_call | solution.py:95
  62.2 1.9 %collective-permute-done.5 = f32[4,32,128]{2,1,0:T(8,128)S(1)} collective-permute-done((f32[4,32,128]{2,1,0:T(8,128)}, f32[4,32,128]{2,1,0:T(8,128)S(1)}, u32[]{:S(2)}, u32[]{:S(2)}) %collective-permute-start.5) | collective-permute-done | bytes 65568 | tf_op jit(solution)/shard_map/ppermute | solution.py:124
  64.2 0.0 copy-done
  64.2 0.9 %fusion = bf16[32,4,128]{2,0,1:T(8,128)(2,1)S(1)} fusion(f32[4,32,128]{2,1,0:T(8,128)} %conv_keep.1, f32[4,32,128]{2,1,0:T(8,128)S(1)} %collective-permute-done.5, f32[32]{0:T(128)S(1)} %copy-done), kind=kLoop, calls=%fused_computation.4 | loop fusion | flops 49152 | bytes 163968 | tf_op jit(solution)/shard_map/transpose | solution.py:126
  65.1 0.6 copy.5
  (2 shorter events, 0.0 us)
Async XLA Ops:
  1.7 44.3 %all-to-all-start = ((bf16[16,4,32,128]{3,2,1,0:T(8,128)(2,1)}), bf16[16,4,32,128]{3,2,1,0:T(8,128)(2,1)S(1)}, u32[]{:S(2)}, u32[]{:S(2)}) async-start(bf16[16,4,32,128]{3,2,1,0:T(8,128)(2,1)} %spread.1), calls=%async_computation | async-start | bytes 1048576 | tf_op jit(solution)/shard_map/all_to_all | solution.py:107
  18.6 6.8 %collective-permute-start.1 = (bf16[432,128]{1,0:T(8,128)(2,1)}, bf16[432,128]{1,0:T(8,128)(2,1)S(1)}, u32[]{:S(2)}, u32[]{:S(2)}) collective-permute-start(bf16[432,128]{1,0:T(8,128)(2,1)} %pack.1), channel_id=1, source_target_pairs={{16,0},{272,16},{0,256},{256,272},{17,1},{273,17},{1,257},{257,273... | collective-permute-start | bytes 331784 | tf_op jit(solution)/shard_map/ppermute | solution.py:112
  21.9 3.5 %collective-permute-start = (bf16[432,128]{1,0:T(8,128)(2,1)}, bf16[432,128]{1,0:T(8,128)(2,1)S(1)}, u32[]{:S(2)}, u32[]{:S(2)}) collective-permute-start(bf16[432,128]{1,0:T(8,128)(2,1)} %pack.1), channel_id=1, source_target_pairs={{0,0},{256,16},{16,256},{272,272},{1,1},{257,17},{17,257},{273,273... | collective-permute-start | bytes 331784 | tf_op jit(solution)/shard_map/ppermute | solution.py:112
  39.8 13.4 %collective-permute-start.2 = (bf16[4,2,432,128]{3,2,1,0:T(8,128)(2,1)S(1)}, bf16[4,2,432,128]{3,2,1,0:T(8,128)(2,1)S(1)}, u32[]{:S(2)}, u32[]{:S(2)}) collective-permute-start(bf16[4,2,432,128]{3,2,1,0:T(8,128)(2,1)S(1)} %bitcast.9), channel_id=1, source_target_pairs={{0,32},{32,0},{1,33},{33,1},{2,34},{34,2},{3,35},{35,3},{4,36},{36... | collective-permute-start | bytes 2654216 | tf_op jit(solution)/shard_map/ppermute | solution.py:115
  46.0 9.9 %collective-permute-start.4 = (bf16[16,32,128]{2,1,0:T(8,128)(2,1)S(1)}, bf16[16,32,128]{2,1,0:T(8,128)(2,1)S(1)}, u32[]{:S(2)}, u32[]{:S(2)}) collective-permute-start(bf16[16,32,128]{2,1,0:T(8,128)(2,1)S(1)} %get-tuple-element.5), channel_id=1, source_target_pairs={{32,64},{64,32},{96,128},{128,96},{160,192},{192,160},{224,256},{2... | collective-permute-start | bytes 393224 | tf_op jit(solution)/shard_map/ppermute | solution.py:120
  51.2 4.7 %collective-permute-start.3 = (bf16[16,32,128]{2,1,0:T(8,128)(2,1)S(1)}, bf16[16,32,128]{2,1,0:T(8,128)(2,1)S(1)}, u32[]{:S(2)}, u32[]{:S(2)}) collective-permute-start(bf16[16,32,128]{2,1,0:T(8,128)(2,1)S(1)} %get-tuple-element.6), channel_id=1, source_target_pairs={{0,32},{32,0},{1,33},{33,1},{2,34},{34,2},{3,35},{35,3},{4,36},{36... | collective-permute-start | bytes 393224 | tf_op jit(solution)/shard_map/ppermute | solution.py:121
  57.7 6.5 %copy-start = (f32[32]{0:T(128)S(1)}, f32[32]{0:T(128)}, u32[]{:S(2)}) copy-start(f32[32]{0:T(128)} %param.5) | copy-start | bytes 388
  57.7 6.5 %collective-permute-start.5 = (f32[4,32,128]{2,1,0:T(8,128)}, f32[4,32,128]{2,1,0:T(8,128)S(1)}, u32[]{:S(2)}, u32[]{:S(2)}) collective-permute-start(f32[4,32,128]{2,1,0:T(8,128)} %conv_send.1), channel_id=1, source_target_pairs={{0,16},{16,0},{1,17},{17,1},{2,18},{18,2},{3,19},{19,3},{4,20},{20... | collective-permute-start | bytes 196616 | tf_op jit(solution)/shard_map/ppermute | solution.py:124

commit v3 on v2

v3 whole, which is shorter than its diff:
```python
import jax
import jax.numpy as jnp
from jax import lax
from jax.experimental import pallas as pl
from jax.experimental.pallas import tpu as pltpu
from jax.sharding import Mesh, PartitionSpec as P


AXES = ("xh", "y", "core", "xl", "z")
LANES = 128
TAPS = 27
FILT = 32
ROWS = TAPS * FILT
HALF = ROWS // 2
VM = pl.BlockSpec(memory_space=pltpu.VMEM)


def order_rows(x, outer):
    inner = 128 // outer
    i = lax.broadcasted_iota(jnp.int32, (128, 128), 0)
    j = lax.broadcasted_iota(jnp.int32, (128, 128), 1)
    pick = (j == lax.rem(i, inner) * outer + lax.div(i, inner)).astype(jnp.bfloat16)
    return jnp.dot(pick, x, preferred_element_type=jnp.float32).astype(jnp.bfloat16)


def spread_kernel(x_ref, o_ref):
    planes = order_rows(x_ref[...], 4).reshape(4, FILT, LANES)
    for z in range(16):
        o_ref[z] = planes


def spread(volume):
    return pl.pallas_call(
        spread_kernel,
        out_shape=jax.ShapeDtypeStruct((16, 4, FILT, LANES), jnp.bfloat16),
        in_specs=[VM],
        out_specs=VM,
        name="spread",
    )(volume.reshape(4 * FILT, LANES))


def finish_kernel(keep_ref, other_ref, column_ref, o_ref):
    total = (keep_ref[...] + other_ref[1 - lax.axis_index("xl")] + column_ref[...]).astype(jnp.bfloat16)
    o_ref[...] = order_rows(total.reshape(4 * FILT, LANES), FILT)


def finish(keep, other, column):
    return pl.pallas_call(
        finish_kernel,
        out_shape=jax.ShapeDtypeStruct((4 * FILT, LANES), jnp.bfloat16),
        in_specs=[VM] * 3,
        out_specs=VM,
        name="finish",
    )(keep, other, column).reshape(FILT, 4, LANES)


def pack_kernel(w_ref, bias_ref, o_ref, column_ref):
    w = w_ref[...].reshape(ROWS, 64)
    o_ref[...] = jnp.concatenate([w[:HALF], w[HALF:]], axis=1)
    i = lax.broadcasted_iota(jnp.int32, (FILT, FILT), 0)
    j = lax.broadcasted_iota(jnp.int32, (FILT, FILT), 1)
    column = jnp.sum(jnp.where(i == j, bias_ref[...], 0.0), axis=1, keepdims=True)
    column_ref[...] = jnp.broadcast_to(column, (FILT, LANES))


def pack(kernel, bias):
    return pl.pallas_call(
        pack_kernel,
        out_shape=[jax.ShapeDtypeStruct((HALF, LANES), jnp.bfloat16), pltpu.VMEM((FILT, LANES), jnp.float32)],
        in_specs=[VM] * 2,
        out_specs=[VM] * 2,
        name="pack",
    )(kernel, bias)


def conv_kernel(own_ref, pair_ref, x_ref, near_ref, far_ref, send_ref, keep_ref, xs, zs):
    core = lax.axis_index("core")
    slot = lax.axis_index("xl") ^ lax.axis_index("xh")
    for dy in range(4):
        q = dy
        for part in range(2):
            rows = slice(dy * 128 + part * 64, dy * 128 + part * 64 + 64)
            z = pl.ds(4 * q + 2 * (core ^ part), 2)
            xs[rows, pl.ds(pl.multiple_of(640 * (1 - core), 128), 128)] = near_ref[z].reshape(64, LANES)
            xs[rows, pl.ds(pl.multiple_of(640 * core, 128), 128)] = far_ref[z].reshape(64, LANES)
            for d in range(4):
                xs[rows, (d + 1) * 128 : (d + 2) * 128] = x_ref[z, d].reshape(64, LANES)
    lane = lax.broadcasted_iota(jnp.int32, (FILT, LANES), 1)
    row, cell = lane // 32, lane % 32
    for flip, o_ref in ((1, send_ref), (0, keep_ref)):
        group = slot ^ flip
        first = []
        second = []
        for dy in range(4):
            a = own_ref[dy, group]
            b = pair_ref[dy, group]
            first.append(jnp.concatenate([a[:, :64], b[:, :64]], axis=1))
            second.append(jnp.concatenate([a[:, 64:], b[:, 64:]], axis=1))
        first = jnp.concatenate(first, axis=1)
        second = jnp.concatenate(second, axis=1)
        for part in range(2):
            lead = 144 * part
            blocks = (
                first[lead : lead + 144],
                (second[0:144] if part else first[288:432]),
                second[lead + 144 : lead + 288],
            )
            zs[lead : lead + 144] = sum(
                jnp.dot(w, xs[:, 128 * a : 128 * a + 512], preferred_element_type=jnp.float32) for a, w in enumerate(blocks)
            )
        for d in range(4):
            total = None
            for b in range(3):
                for e in range(3):
                    at = (3 * b + e) * FILT
                    part = zs[at : at + FILT, d * 128 : (d + 1) * 128]
                    shift = (b - 1) * 32 + (e - 1)
                    if shift != 0:
                        part = pltpu.roll(part, (-shift) % LANES, 1)
                        ok = (row + (b - 1) >= 0) & (row + (b - 1) < 4) & (cell + (e - 1) >= 0) & (cell + (e - 1) < 32)
                        part = jnp.where(ok, part, 0.0)
                    total = part if total is None else total + part
            o_ref[d] = total


def conv(own, pair, x, near, far):
    return pl.pallas_call(
        conv_kernel,
        out_shape=[pltpu.VMEM((4, FILT, LANES), jnp.float32)] * 2,
        in_specs=[VM] * 5,
        out_specs=[VM] * 2,
        scratch_shapes=[pltpu.VMEM((512, 768), jnp.bfloat16), pltpu.VMEM((ROWS // 3, 512), jnp.float32)],
        name="conv",
    )(own, pair, x, near, far)


def work(volume, kernel, bias):
    spread_x = spread(volume)
    x_all = lax.all_to_all(spread_x, "z", 0, 0, tiled=True)
    kernel, bias = (pltpu.with_memory_space_constraint(v, pltpu.VMEM) for v in (kernel, bias.reshape(1, FILT)))
    packed, column = pack(kernel, bias)
    turned = []
    for r in range(2):
        pairs = [(2 * tl + (th + r) % 2, 2 * th + tl) for th in range(2) for tl in range(2)]
        turned.append(lax.ppermute(packed, ("xh", "xl"), pairs))
    both = jnp.stack(turned)
    own = lax.all_gather(both, "y", axis=0, tiled=False)
    pair = lax.ppermute(own, "core", [(0, 1), (1, 0)])
    core = lax.axis_index("core")
    outside = [(i, i - 1) if i % 2 == 0 else (i, i + 1) for i in range(1, 15)]
    near = lax.dynamic_index_in_dim(x_all, 3 * (1 - core), 1, keepdims=False)
    far = lax.dynamic_index_in_dim(x_all, 3 * core, 1, keepdims=False)
    near = lax.ppermute(near, "core", [(0, 1), (1, 0)])
    far = lax.ppermute(far, ("xh", "y", "core"), outside)
    own, pair, x_all, near, far = (pltpu.with_memory_space_constraint(v, pltpu.VMEM) for v in (own, pair, x_all, near, far))
    send, keep = conv(own, pair, x_all, near, far)
    other = lax.all_gather(send, "xl", axis=0, tiled=False)
    keep, other = (pltpu.with_memory_space_constraint(v, pltpu.VMEM) for v in (keep, other))
    return finish(keep, other, pltpu.with_memory_space_constraint(column, pltpu.VMEM))


def solution(mesh):
    fine = Mesh(mesh.devices.reshape(2, 4, 2, 2, 16), AXES)
    vox = ("xh", "y", "core")
    filt = ("xl", "z")
    in_specs = (P(filt, vox, None), P(None, filt, vox), P(filt))
    return jax.shard_map(work, mesh=fine, in_specs=in_specs, out_specs=P(filt, vox, None), check_vma=False)
```

time: 66.2 us -> 63.6 us (0.961)
  the two profiles are of different devices: /device:TPU:6 before, /device:TPU:4 now
where the time goes in v3:
time: 63.6 us; the launch traced here: 63.2 us
  starting transfers between devices  27.8 us (44%)
  blocking collectives  19 us (30%)
  waiting for transfers between devices  11 us (17%)
  Pallas kernels  4.69 us (7%)
  local copies, waits for them, and re-layouts  0.66 us (1%)
    all_to_all x1, starting transfers between devices, work(): x_all = lax.all_to_all(spread_x, 'z', 0, 0, tiled=True)  15.3 us
    all_gather x1, blocking collectives, work(): own = lax.all_gather(both, 'y', axis=0, tiled=False)  14 us
    ppermute x2, waiting for transfers between devices, work(): turned.append(lax.ppermute(packed, ('xh', 'xl'), pairs))  5.6 us
    ppermute x2, starting transfers between devices, work(): turned.append(lax.ppermute(packed, ('xh', 'xl'), pairs))  5.01 us
    all_gather x1, blocking collectives, work(): other = lax.all_gather(send, 'xl', axis=0, tiled=False)  4.93 us
    ppermute x1, waiting for transfers between devices, work(): far = lax.ppermute(far, ('xh', 'y', 'core'), outside)  4.37 us
    ppermute x1, starting transfers between devices, work(): near = lax.ppermute(near, 'core', [(0, 1), (1, 0)])  3.59 us
    ppermute x1, starting transfers between devices, work(): far = lax.ppermute(far, ('xh', 'y', 'core'), outside)  1.92 us
  transfers between devices with their start and end apart: 6, of which 4 were waited for; matrix products, arithmetic and copies ran while one was open for 0% of the time, Pallas kernels for 1%

profile of v3, /device:TPU:4, one launch (start us, length us, event | category | flops | bytes accessed | tf_op | source)
XLA Modules:
  0.0 63.2 jit_solution(1242144757047628627)
XLA Ops:
  0.0 1.7 %spread.1 = bf16[16,4,32,128]{3,2,1,0:T(8,128)(2,1)} custom-call(bf16[128,128]{1,0:T(8,128)(2,1)} %bitcast.17), custom_call_target="tpu_custom_call" | custom-call | tf_op jit(solution)/shard_map/spread/pallas_call | solution.py:33
  1.7 0.0 copy-start
  1.7 15.3 %all-to-all-start = ((bf16[16,4,32,128]{3,2,1,0:T(8,128)(2,1)}), bf16[16,4,32,128]{3,2,1,0:T(8,128)(2,1)S(1)}, u32[]{:S(2)}, u32[]{:S(2)}) async-start(bf16[16,4,32,128]{3,2,1,0:T(8,128)(2,1)} %spread.1), calls=%async_computation | async-start | bytes 1048576 | tf_op jit(solution)/shard_map/all_to_all | solution.py:139
  17.1 0.0 copy-start.1
  17.1 0.0 copy-done
  17.1 0.6 %copy-done.1 = f32[32]{0:T(128)S(1)} copy-done((f32[32]{0:T(128)S(1)}, f32[32]{0:T(128)}, u32[]{:S(2)}) %copy-start.1) | copy-done | bytes 152
  17.7 0.8 %pack.1 = (bf16[432,128]{1,0:T(8,128)(2,1)}, f32[32,128]{1,0:T(8,128)S(1)}) custom-call(bf16[27,32,64]{2,1,0:T(8,128)(2,1)S(1)} %copy-done, f32[1,32]{1,0:T(1,128)S(1)} %bitcast.14), custom_call_target="tpu_custom_call" | custom-call | tf_op jit(solution)/shard_map/pack/pallas_call | solution.py:67
  18.5 3.1 %collective-permute-start.1 = (bf16[432,128]{1,0:T(8,128)(2,1)}, bf16[432,128]{1,0:T(8,128)(2,1)S(1)}, u32[]{:S(2)}, u32[]{:S(2)}) collective-permute-start(bf16[432,128]{1,0:T(8,128)(2,1)} %get-tuple-element.9), channel_id=1, source_target_pairs={{16,0},{272,16},{0,256},{256,272},{17,1},{273,17},{1,257},{257,273... | collective-permute-start | bytes 331784 | tf_op jit(solution)/shard_map/ppermute | solution.py:145
  21.6 1.9 %collective-permute-start = (bf16[432,128]{1,0:T(8,128)(2,1)}, bf16[432,128]{1,0:T(8,128)(2,1)S(1)}, u32[]{:S(2)}, u32[]{:S(2)}) collective-permute-start(bf16[432,128]{1,0:T(8,128)(2,1)} %get-tuple-element.9), channel_id=1, source_target_pairs={{0,0},{256,16},{16,256},{272,272},{1,1},{257,17},{17,257},{273,273... | collective-permute-start | bytes 331784 | tf_op jit(solution)/shard_map/ppermute | solution.py:145
  23.5 3.4 %collective-permute-done.1 = bf16[432,128]{1,0:T(8,128)(2,1)S(1)} collective-permute-done((bf16[432,128]{1,0:T(8,128)(2,1)}, bf16[432,128]{1,0:T(8,128)(2,1)S(1)}, u32[]{:S(2)}, u32[]{:S(2)}) %collective-permute-start.1) | collective-permute-done | bytes 110624 | tf_op jit(solution)/shard_map/ppermute | solution.py:145
  26.9 2.2 %collective-permute-done = bf16[432,128]{1,0:T(8,128)(2,1)S(1)} collective-permute-done((bf16[432,128]{1,0:T(8,128)(2,1)}, bf16[432,128]{1,0:T(8,128)(2,1)S(1)}, u32[]{:S(2)}, u32[]{:S(2)}) %collective-permute-start) | collective-permute-done | bytes 110624 | tf_op jit(solution)/shard_map/ppermute | solution.py:145
  29.1 14.0 %all-gather = bf16[8,432,128]{2,1,0:T(8,128)(2,1)S(1)} all-gather(bf16[2,432,128]{2,1,0:T(8,128)(2,1)S(1)} %pad_maximum_fusion), channel_id=2, replica_groups=mesh['xh'=2,'y'=4,'core'=2,'xl'=2,'z'=16] {'y'}, dimensions={0}, use_global_device_ids=true | all-gather | bytes 1105920 | tf_op jit(solution)/shard_map/all_gather | solution.py:147
  43.2 1.9 %collective-permute-start.2 = (bf16[4,2,432,128]{3,2,1,0:T(8,128)(2,1)S(1)}, bf16[4,2,432,128]{3,2,1,0:T(8,128)(2,1)S(1)}, u32[]{:S(2)}, u32[]{:S(2)}) collective-permute-start(bf16[4,2,432,128]{3,2,1,0:T(8,128)(2,1)S(1)} %bitcast.11), channel_id=1, source_target_pairs={{0,32},{32,0},{1,33},{33,1},{2,34},{34,2},{3,35},{35,3},{4,36},{36... | collective-permute-start | bytes 2654216 | tf_op jit(solution)/shard_map/ppermute | solution.py:148
  45.1 1.0 %all-to-all-done.x_ref = bf16[16,4,32,128]{3,2,1,0:T(8,128)(2,1)S(1)} async-done(((bf16[16,4,32,128]{3,2,1,0:T(8,128)(2,1)}), bf16[16,4,32,128]{3,2,1,0:T(8,128)(2,1)S(1)}, u32[]{:S(2)}, u32[]{:S(2)}) %all-to-all-start) | async-done | bytes 524320 | tf_op jit(solution)/shard_map/all_to_all | solution.py:139
  46.2 1.9 %collective-permute-start.4 = (bf16[16,32,128]{2,1,0:T(8,128)(2,1)S(1)}, bf16[16,32,128]{2,1,0:T(8,128)(2,1)S(1)}, u32[]{:S(2)}, u32[]{:S(2)}) collective-permute-start(bf16[16,32,128]{2,1,0:T(8,128)(2,1)S(1)} %get-tuple-element.13), channel_id=1, source_target_pairs={{32,64},{64,32},{96,128},{128,96},{160,192},{192,160},{224,256},{2... | collective-permute-start | bytes 393224 | tf_op jit(solution)/shard_map/ppermute | solution.py:154
  48.1 3.6 %collective-permute-start.3 = (bf16[16,32,128]{2,1,0:T(8,128)(2,1)S(1)}, bf16[16,32,128]{2,1,0:T(8,128)(2,1)S(1)}, u32[]{:S(2)}, u32[]{:S(2)}) collective-permute-start(bf16[16,32,128]{2,1,0:T(8,128)(2,1)S(1)} %get-tuple-element.14), channel_id=1, source_target_pairs={{0,32},{32,0},{1,33},{33,1},{2,34},{34,2},{3,35},{35,3},{4,36},{36... | collective-permute-start | bytes 393224 | tf_op jit(solution)/shard_map/ppermute | solution.py:153
  51.7 0.0 collective-permute-done.2.pair_ref
  51.7 4.4 %collective-permute-done.4.far_ref = bf16[16,32,128]{2,1,0:T(8,128)(2,1)S(1)} collective-permute-done((bf16[16,32,128]{2,1,0:T(8,128)(2,1)S(1)}, bf16[16,32,128]{2,1,0:T(8,128)(2,1)S(1)}, u32[]{:S(2)}, u32[]{:S(2)}) %collective-permute-start.4) | collective-permute-done | bytes 131104 | tf_op jit(solution)/shard_map/ppermute | solution.py:154
  56.1 0.0 collective-permute-done.3.near_ref
  56.1 1.4 %conv.1 = (f32[4,32,128]{2,1,0:T(8,128)S(1)}, f32[4,32,128]{2,1,0:T(8,128)S(1)}) custom-call(bf16[4,2,432,128]{3,2,1,0:T(8,128)(2,1)S(1)} %bitcast.12, bf16[4,2,432,128]{3,2,1,0:T(8,128)(2,1)S(1)} %collective-permute-done.2.pair_ref, bf16[16,4,32,128]{3,2,1,0:T(8,128)(2,1)S(1)} %all-to-all-done.x_ref, ...), custom_call_target="tpu_custom_call" | custom-call | tf_op jit(solution)/shard_map/conv/pallas_call | solution.py:127
  57.5 4.9 %all-gather.1 = f32[8,32,128]{2,1,0:T(8,128)S(1)} all-gather(f32[4,32,128]{2,1,0:T(8,128)S(1)} %get-tuple-element.11), channel_id=3, replica_groups=mesh['xh'=2,'y'=4,'core'=2,'xl'=2,'z'=16] {'xl'}, dimensions={0}, use_global_device_ids=true | all-gather | bytes 196608 | tf_op jit(solution)/shard_map/all_gather | solution.py:157
  62.5 0.8 %finish.1 = bf16[128,128]{1,0:T(8,128)(2,1)} custom-call(f32[4,32,128]{2,1,0:T(8,128)S(1)} %get-tuple-element.10.keep_ref, f32[2,4,32,128]{3,2,1,0:T(8,128)S(1)} %bitcast.13, f32[32,128]{1,0:T(8,128)S(1)} %get-tuple-element.12.column_ref), custom_call_target="tpu_custom_call" | custom-call | tf_op jit(solution)/shard_map/finish/pallas_call | solution.py:48
  (2 shorter events, 0.0 us)
Async XLA Ops:
  1.7 15.4 %copy-start = (bf16[27,32,64]{2,1,0:T(8,128)(2,1)S(1)}, bf16[27,32,64]{2,1,0:T(8,128)(2,1)}, u32[]{:S(2)}) copy-start(bf16[27,32,64]{2,1,0:T(8,128)(2,1)} %w_ref.1) | copy-start | bytes 331780
  1.7 44.4 %all-to-all-start = ((bf16[16,4,32,128]{3,2,1,0:T(8,128)(2,1)}), bf16[16,4,32,128]{3,2,1,0:T(8,128)(2,1)S(1)}, u32[]{:S(2)}, u32[]{:S(2)}) async-start(bf16[16,4,32,128]{3,2,1,0:T(8,128)(2,1)} %spread.1), calls=%async_computation | async-start | bytes 1048576 | tf_op jit(solution)/shard_map/all_to_all | solution.py:139
  17.1 0.7 %copy-start.1 = (f32[32]{0:T(128)S(1)}, f32[32]{0:T(128)}, u32[]{:S(2)}) copy-start(f32[32]{0:T(128)} %param.5) | copy-start | bytes 388
  18.5 8.4 %collective-permute-start.1 = (bf16[432,128]{1,0:T(8,128)(2,1)}, bf16[432,128]{1,0:T(8,128)(2,1)S(1)}, u32[]{:S(2)}, u32[]{:S(2)}) collective-permute-start(bf16[432,128]{1,0:T(8,128)(2,1)} %get-tuple-element.9), channel_id=1, source_target_pairs={{16,0},{272,16},{0,256},{256,272},{17,1},{273,17},{1,257},{257,273... | collective-permute-start | bytes 331784 | tf_op jit(solution)/shard_map/ppermute | solution.py:145
  21.6 7.5 %collective-permute-start = (bf16[432,128]{1,0:T(8,128)(2,1)}, bf16[432,128]{1,0:T(8,128)(2,1)S(1)}, u32[]{:S(2)}, u32[]{:S(2)}) collective-permute-start(bf16[432,128]{1,0:T(8,128)(2,1)} %get-tuple-element.9), channel_id=1, source_target_pairs={{0,0},{256,16},{16,256},{272,272},{1,1},{257,17},{17,257},{273,273... | collective-permute-start | bytes 331784 | tf_op jit(solution)/shard_map/ppermute | solution.py:145
  43.2 8.5 %collective-permute-start.2 = (bf16[4,2,432,128]{3,2,1,0:T(8,128)(2,1)S(1)}, bf16[4,2,432,128]{3,2,1,0:T(8,128)(2,1)S(1)}, u32[]{:S(2)}, u32[]{:S(2)}) collective-permute-start(bf16[4,2,432,128]{3,2,1,0:T(8,128)(2,1)S(1)} %bitcast.11), channel_id=1, source_target_pairs={{0,32},{32,0},{1,33},{33,1},{2,34},{34,2},{3,35},{35,3},{4,36},{36... | collective-permute-start | bytes 2654216 | tf_op jit(solution)/shard_map/ppermute | solution.py:148
  46.2 9.9 %collective-permute-start.4 = (bf16[16,32,128]{2,1,0:T(8,128)(2,1)S(1)}, bf16[16,32,128]{2,1,0:T(8,128)(2,1)S(1)}, u32[]{:S(2)}, u32[]{:S(2)}) collective-permute-start(bf16[16,32,128]{2,1,0:T(8,128)(2,1)S(1)} %get-tuple-element.13), channel_id=1, source_target_pairs={{32,64},{64,32},{96,128},{128,96},{160,192},{192,160},{224,256},{2... | collective-permute-start | bytes 393224 | tf_op jit(solution)/shard_map/ppermute | solution.py:154
  48.1 8.0 %collective-permute-start.3 = (bf16[16,32,128]{2,1,0:T(8,128)(2,1)S(1)}, bf16[16,32,128]{2,1,0:T(8,128)(2,1)S(1)}, u32[]{:S(2)}, u32[]{:S(2)}) collective-permute-start(bf16[16,32,128]{2,1,0:T(8,128)(2,1)S(1)} %get-tuple-element.14), channel_id=1, source_target_pairs={{0,32},{32,0},{1,33},{33,1},{2,34},{34,2},{3,35},{35,3},{4,36},{36... | collective-permute-start | bytes 393224 | tf_op jit(solution)/shard_map/ppermute | solution.py:153

commit v4 on v3

--- a/solution.py
+++ b/solution.py
@@ -32,11 +32,11 @@
 def spread(volume):
     return pl.pallas_call(
         spread_kernel,
-        out_shape=jax.ShapeDtypeStruct((16, 4, FILT, LANES), jnp.bfloat16),
+        out_shape=pltpu.VMEM((16, 4, FILT, LANES), jnp.bfloat16),
         in_specs=[VM],
         out_specs=VM,
         name="spread",
-    )(volume.reshape(4 * FILT, LANES))
+    )(pltpu.with_memory_space_constraint(volume.reshape(4 * FILT, LANES), pltpu.VMEM))
 
 
 def finish_kernel(keep_ref, other_ref, column_ref, o_ref):
@@ -81,7 +81,7 @@
         for part in range(2):
             rows = slice(dy * 128 + part * 64, dy * 128 + part * 64 + 64)
             z = pl.ds(4 * q + 2 * (core ^ part), 2)
-            xs[rows, pl.ds(pl.multiple_of(640 * (1 - core), 128), 128)] = near_ref[z].reshape(64, LANES)
+            xs[rows, pl.ds(pl.multiple_of(640 * (1 - core), 128), 128)] = near_ref[1 - core, z].reshape(64, LANES)
             xs[rows, pl.ds(pl.multiple_of(640 * core, 128), 128)] = far_ref[z].reshape(64, LANES)
             for d in range(4):
                 xs[rows, (d + 1) * 128 : (d + 2) * 128] = x_ref[z, d].reshape(64, LANES)
@@ -150,7 +150,7 @@
     outside = [(i, i - 1) if i % 2 == 0 else (i, i + 1) for i in range(1, 15)]
     near = lax.dynamic_index_in_dim(x_all, 3 * (1 - core), 1, keepdims=False)
     far = lax.dynamic_index_in_dim(x_all, 3 * core, 1, keepdims=False)
-    near = lax.ppermute(near, "core", [(0, 1), (1, 0)])
+    near = lax.all_gather(near, "core", axis=0, tiled=False)
     far = lax.ppermute(far, ("xh", "y", "core"), outside)
     own, pair, x_all, near, far = (pltpu.with_memory_space_constraint(v, pltpu.VMEM) for v in (own, pair, x_all, near, far))
     send, keep = conv(own, pair, x_all, near, far)

time: 63.6 us -> 63.6 us (level)
  starting transfers between devices: 27.8 us -> 24.2 us
  blocking collectives: 19 us -> 22.3 us
  Pallas kernels: 4.69 us -> 3.93 us
  local copies, waits for them, and re-layouts: 0.66 us -> 1.42 us
    ppermute x1 -> x0, starting transfers between devices: 3.59 us -> none  [work(): near = lax.ppermute(near, 'core', [(0, 1), (1, 0)])]
    all_gather x0 -> x1, blocking collectives: none -> 3.31 us  [work(): near = lax.all_gather(near, 'core', axis=0, tiled=False)]
    unnamed x4 -> x6, local copies, waits for them, and re-layouts: 0.64 us -> 1.4 us
    pallas_call x1, Pallas kernels: 1.74 us -> 0.98 us  [spread(): pl.pallas_call(spread_kernel, out_shape=pltpu.VMEM((16, 4, FILT, LANES),...]
  transfers between devices with their start and end apart: 6 -> 5, of which waited for: 4 -> 4; matrix products, arithmetic and copies ran while one was open for 0% -> 0% of each run, Pallas kernels for 1% -> 1%
where the time goes in v4:
time: 63.6 us; the launch traced here: 63.2 us
  starting transfers between devices  24.2 us (38%)
  blocking collectives  22.3 us (35%)
  waiting for transfers between devices  11.3 us (18%)
  Pallas kernels  3.93 us (6%)
  local copies, waits for them, and re-layouts  1.42 us (2%)
    all_to_all x1, starting transfers between devices, work(): x_all = lax.all_to_all(spread_x, 'z', 0, 0, tiled=True)  15.3 us
    all_gather x1, blocking collectives, work(): own = lax.all_gather(both, 'y', axis=0, tiled=False)  14 us
    ppermute x2, waiting for transfers between devices, work(): turned.append(lax.ppermute(packed, ('xh', 'xl'), pairs))  5.6 us
    ppermute x2, starting transfers between devices, work(): turned.append(lax.ppermute(packed, ('xh', 'xl'), pairs))  5.01 us
    all_gather x1, blocking collectives, work(): other = lax.all_gather(send, 'xl', axis=0, tiled=False)  4.93 us
    ppermute x1, waiting for transfers between devices, work(): far = lax.ppermute(far, ('xh', 'y', 'core'), outside)  4.66 us
    all_gather x1, blocking collectives, work(): near = lax.all_gather(near, 'core', axis=0, tiled=False)  3.31 us
    ppermute x1, starting transfers between devices, work(): far = lax.ppermute(far, ('xh', 'y', 'core'), outside)  1.92 us
  transfers between devices with their start and end apart: 5, of which 4 were waited for; matrix products, arithmetic and copies ran while one was open for 0% of the time, Pallas kernels for 1%

profile of v4, /device:TPU:4, one launch (start us, length us, event | category | flops | bytes accessed | tf_op | source)
XLA Modules:
  0.0 63.2 jit_solution(15921950460032807880)
XLA Ops:
  0.0 0.0 copy-start.1
  0.0 0.8 %copy-done.1 = bf16[32,4,128]{2,1,0:T(4,128)(2,1)S(1)} copy-done((bf16[32,4,128]{2,1,0:T(4,128)(2,1)S(1)}, bf16[32,4,128]{2,1,0:T(4,128)(2,1)}, u32[]{:S(2)}) %copy-start.1) | copy-done | bytes 32792
  0.8 1.0 %spread.1 = bf16[16,4,32,128]{3,2,1,0:T(8,128)(2,1)} custom-call(bf16[128,128]{1,0:T(8,128)(2,1)S(1)} %bitcast.14), custom_call_target="tpu_custom_call" | custom-call | tf_op jit(solution)/shard_map/spread/pallas_call | solution.py:33
  1.7 0.0 copy-start
  1.7 15.3 %all-to-all-start = ((bf16[16,4,32,128]{3,2,1,0:T(8,128)(2,1)}), bf16[16,4,32,128]{3,2,1,0:T(8,128)(2,1)S(1)}, u32[]{:S(2)}, u32[]{:S(2)}) async-start(bf16[16,4,32,128]{3,2,1,0:T(8,128)(2,1)} %spread.1), calls=%async_computation | async-start | bytes 1048576 | tf_op jit(solution)/shard_map/all_to_all | solution.py:139
  17.1 0.0 copy-start.2
  17.1 0.0 copy-done
  17.1 0.6 %copy-done.2 = f32[32]{0:T(128)S(1)} copy-done((f32[32]{0:T(128)S(1)}, f32[32]{0:T(128)}, u32[]{:S(2)}) %copy-start.2) | copy-done | bytes 152
  17.7 0.8 %pack.1 = (bf16[432,128]{1,0:T(8,128)(2,1)}, f32[32,128]{1,0:T(8,128)S(1)}) custom-call(bf16[27,32,64]{2,1,0:T(8,128)(2,1)S(1)} %copy-done, f32[1,32]{1,0:T(1,128)S(1)} %bitcast.15), custom_call_target="tpu_custom_call" | custom-call | tf_op jit(solution)/shard_map/pack/pallas_call | solution.py:67
  18.5 3.1 %collective-permute-start.1 = (bf16[432,128]{1,0:T(8,128)(2,1)}, bf16[432,128]{1,0:T(8,128)(2,1)S(1)}, u32[]{:S(2)}, u32[]{:S(2)}) collective-permute-start(bf16[432,128]{1,0:T(8,128)(2,1)} %get-tuple-element.9), channel_id=1, source_target_pairs={{16,0},{272,16},{0,256},{256,272},{17,1},{273,17},{1,257},{257,273... | collective-permute-start | bytes 331784 | tf_op jit(solution)/shard_map/ppermute | solution.py:145
  21.6 1.9 %collective-permute-start = (bf16[432,128]{1,0:T(8,128)(2,1)}, bf16[432,128]{1,0:T(8,128)(2,1)S(1)}, u32[]{:S(2)}, u32[]{:S(2)}) collective-permute-start(bf16[432,128]{1,0:T(8,128)(2,1)} %get-tuple-element.9), channel_id=1, source_target_pairs={{0,0},{256,16},{16,256},{272,272},{1,1},{257,17},{17,257},{273,273... | collective-permute-start | bytes 331784 | tf_op jit(solution)/shard_map/ppermute | solution.py:145
  23.5 3.4 %collective-permute-done.1 = bf16[432,128]{1,0:T(8,128)(2,1)S(1)} collective-permute-done((bf16[432,128]{1,0:T(8,128)(2,1)}, bf16[432,128]{1,0:T(8,128)(2,1)S(1)}, u32[]{:S(2)}, u32[]{:S(2)}) %collective-permute-start.1) | collective-permute-done | bytes 110624 | tf_op jit(solution)/shard_map/ppermute | solution.py:145
  26.9 2.2 %collective-permute-done = bf16[432,128]{1,0:T(8,128)(2,1)S(1)} collective-permute-done((bf16[432,128]{1,0:T(8,128)(2,1)}, bf16[432,128]{1,0:T(8,128)(2,1)S(1)}, u32[]{:S(2)}, u32[]{:S(2)}) %collective-permute-start) | collective-permute-done | bytes 110624 | tf_op jit(solution)/shard_map/ppermute | solution.py:145
  29.1 14.0 %all-gather = bf16[8,432,128]{2,1,0:T(8,128)(2,1)S(1)} all-gather(bf16[2,432,128]{2,1,0:T(8,128)(2,1)S(1)} %pad_maximum_fusion), channel_id=2, replica_groups=mesh['xh'=2,'y'=4,'core'=2,'xl'=2,'z'=16] {'y'}, dimensions={0}, use_global_device_ids=true | all-gather | bytes 1105920 | tf_op jit(solution)/shard_map/all_gather | solution.py:147
  43.2 1.9 %collective-permute-start.2 = (bf16[4,2,432,128]{3,2,1,0:T(8,128)(2,1)S(1)}, bf16[4,2,432,128]{3,2,1,0:T(8,128)(2,1)S(1)}, u32[]{:S(2)}, u32[]{:S(2)}) collective-permute-start(bf16[4,2,432,128]{3,2,1,0:T(8,128)(2,1)S(1)} %bitcast.10), channel_id=1, source_target_pairs={{0,32},{32,0},{1,33},{33,1},{2,34},{34,2},{3,35},{35,3},{4,36},{36... | collective-permute-start | bytes 2654216 | tf_op jit(solution)/shard_map/ppermute | solution.py:148
  45.1 1.0 %all-to-all-done.x_ref = bf16[16,4,32,128]{3,2,1,0:T(8,128)(2,1)S(1)} async-done(((bf16[16,4,32,128]{3,2,1,0:T(8,128)(2,1)}), bf16[16,4,32,128]{3,2,1,0:T(8,128)(2,1)S(1)}, u32[]{:S(2)}, u32[]{:S(2)}) %all-to-all-start) | async-done | bytes 524320 | tf_op jit(solution)/shard_map/all_to_all | solution.py:139
  46.2 1.9 %collective-permute-start.3 = (bf16[16,32,128]{2,1,0:T(8,128)(2,1)S(1)}, bf16[16,32,128]{2,1,0:T(8,128)(2,1)S(1)}, u32[]{:S(2)}, u32[]{:S(2)}) collective-permute-start(bf16[16,32,128]{2,1,0:T(8,128)(2,1)S(1)} %get-tuple-element.13), channel_id=1, source_target_pairs={{32,64},{64,32},{96,128},{128,96},{160,192},{192,160},{224,256},{2... | collective-permute-start | bytes 393224 | tf_op jit(solution)/shard_map/ppermute | solution.py:154
  48.1 3.3 %all-gather.1 = bf16[32,1,32,128]{3,2,1,0:T(8,128)(2,1)S(1)} all-gather(bf16[16,1,32,128]{3,2,1,0:T(8,128)(2,1)S(1)} %get-tuple-element.14), channel_id=3, replica_groups=mesh['xh'=2,'y'=4,'core'=2,'xl'=2,'z'=16] {'core'}, dimensions={0}, use_global_device_ids=true | all-gather | bytes 393216 | tf_op jit(solution)/shard_map/all_gather | solution.py:153
  51.4 0.0 collective-permute-done.2.pair_ref
  51.4 4.7 %collective-permute-done.3.far_ref = bf16[16,32,128]{2,1,0:T(8,128)(2,1)S(1)} collective-permute-done((bf16[16,32,128]{2,1,0:T(8,128)(2,1)S(1)}, bf16[16,32,128]{2,1,0:T(8,128)(2,1)S(1)}, u32[]{:S(2)}, u32[]{:S(2)}) %collective-permute-start.3) | collective-permute-done | bytes 131104 | tf_op jit(solution)/shard_map/ppermute | solution.py:154
  56.1 1.4 %conv.1 = (f32[4,32,128]{2,1,0:T(8,128)S(1)}, f32[4,32,128]{2,1,0:T(8,128)S(1)}) custom-call(bf16[4,2,432,128]{3,2,1,0:T(8,128)(2,1)S(1)} %bitcast.11, bf16[4,2,432,128]{3,2,1,0:T(8,128)(2,1)S(1)} %collective-permute-done.2.pair_ref, bf16[16,4,32,128]{3,2,1,0:T(8,128)(2,1)S(1)} %all-to-all-done.x_ref, bf16[2,16,32,128]{3,2,1,0:T(8,128)(2,1)S(1)} %bitcast.12, ...), custom_call_target="tpu_custom_call" | custom-call | tf_op jit(solution)/shard_map/conv/pallas_call | solution.py:127
  57.5 4.9 %all-gather.2 = f32[8,32,128]{2,1,0:T(8,128)S(1)} all-gather(f32[4,32,128]{2,1,0:T(8,128)S(1)} %get-tuple-element.11), channel_id=4, replica_groups=mesh['xh'=2,'y'=4,'core'=2,'xl'=2,'z'=16] {'xl'}, dimensions={0}, use_global_device_ids=true | all-gather | bytes 196608 | tf_op jit(solution)/shard_map/all_gather | solution.py:157
  62.4 0.8 %finish.1 = bf16[128,128]{1,0:T(8,128)(2,1)} custom-call(f32[4,32,128]{2,1,0:T(8,128)S(1)} %get-tuple-element.10.keep_ref, f32[2,4,32,128]{3,2,1,0:T(8,128)S(1)} %bitcast.13, f32[32,128]{1,0:T(8,128)S(1)} %get-tuple-element.12.column_ref), custom_call_target="tpu_custom_call" | custom-call | tf_op jit(solution)/shard_map/finish/pallas_call | solution.py:48
  (2 shorter events, 0.0 us)
Async XLA Ops:
  0.0 0.8 %copy-start.1 = (bf16[32,4,128]{2,1,0:T(4,128)(2,1)S(1)}, bf16[32,4,128]{2,1,0:T(4,128)(2,1)}, u32[]{:S(2)}) copy-start(bf16[32,4,128]{2,1,0:T(4,128)(2,1)} %param.3) | copy-start | bytes 98308
  1.7 15.4 %copy-start = (bf16[27,32,64]{2,1,0:T(8,128)(2,1)S(1)}, bf16[27,32,64]{2,1,0:T(8,128)(2,1)}, u32[]{:S(2)}) copy-start(bf16[27,32,64]{2,1,0:T(8,128)(2,1)} %w_ref.1) | copy-start | bytes 331780
  1.7 44.4 %all-to-all-start = ((bf16[16,4,32,128]{3,2,1,0:T(8,128)(2,1)}), bf16[16,4,32,128]{3,2,1,0:T(8,128)(2,1)S(1)}, u32[]{:S(2)}, u32[]{:S(2)}) async-start(bf16[16,4,32,128]{3,2,1,0:T(8,128)(2,1)} %spread.1), calls=%async_computation | async-start | bytes 1048576 | tf_op jit(solution)/shard_map/all_to_all | solution.py:139
  17.1 0.7 %copy-start.2 = (f32[32]{0:T(128)S(1)}, f32[32]{0:T(128)}, u32[]{:S(2)}) copy-start(f32[32]{0:T(128)} %param.5) | copy-start | bytes 388
  18.5 8.4 %collective-permute-start.1 = (bf16[432,128]{1,0:T(8,128)(2,1)}, bf16[432,128]{1,0:T(8,128)(2,1)S(1)}, u32[]{:S(2)}, u32[]{:S(2)}) collective-permute-start(bf16[432,128]{1,0:T(8,128)(2,1)} %get-tuple-element.9), channel_id=1, source_target_pairs={{16,0},{272,16},{0,256},{256,272},{17,1},{273,17},{1,257},{257,273... | collective-permute-start | bytes 331784 | tf_op jit(solution)/shard_map/ppermute | solution.py:145
  21.6 7.5 %collective-permute-start = (bf16[432,128]{1,0:T(8,128)(2,1)}, bf16[432,128]{1,0:T(8,128)(2,1)S(1)}, u32[]{:S(2)}, u32[]{:S(2)}) collective-permute-start(bf16[432,128]{1,0:T(8,128)(2,1)} %get-tuple-element.9), channel_id=1, source_target_pairs={{0,0},{256,16},{16,256},{272,272},{1,1},{257,17},{17,257},{273,273... | collective-permute-start | bytes 331784 | tf_op jit(solution)/shard_map/ppermute | solution.py:145
  43.2 8.2 %collective-permute-start.2 = (bf16[4,2,432,128]{3,2,1,0:T(8,128)(2,1)S(1)}, bf16[4,2,432,128]{3,2,1,0:T(8,128)(2,1)S(1)}, u32[]{:S(2)}, u32[]{:S(2)}) collective-permute-start(bf16[4,2,432,128]{3,2,1,0:T(8,128)(2,1)S(1)} %bitcast.10), channel_id=1, source_target_pairs={{0,32},{32,0},{1,33},{33,1},{2,34},{34,2},{3,35},{35,3},{4,36},{36... | collective-permute-start | bytes 2654216 | tf_op jit(solution)/shard_map/ppermute | solution.py:148
  46.2 9.9 %collective-permute-start.3 = (bf16[16,32,128]{2,1,0:T(8,128)(2,1)S(1)}, bf16[16,32,128]{2,1,0:T(8,128)(2,1)S(1)}, u32[]{:S(2)}, u32[]{:S(2)}) collective-permute-start(bf16[16,32,128]{2,1,0:T(8,128)(2,1)S(1)} %get-tuple-element.13), channel_id=1, source_target_pairs={{32,64},{64,32},{96,128},{128,96},{160,192},{192,160},{224,256},{2... | collective-permute-start | bytes 393224 | tf_op jit(solution)/shard_map/ppermute | solution.py:154
